TPU v7x, 512 devices: a whole 4x4x16 slice. The times are simulated.
512 devices in a mesh: fsdp: 32 (over x, z_lo), member: 16 (over y, z_hi, core).
Axes of the slice: x: 4, y: 4, z: 16 (z_hi: 2, z_lo: 8; z = z_hi * 8 + z_lo), core: 2. Of those that a mesh axis runs over, the one named last changes fastest.
Arguments:
- frames: bfloat16 [16, 4608, 1536], P('member', 'fsdp'), may hold values from -6 to 6
- layer_norm_gain: float32 [1536], replicated, may hold values from 0.25 to 1.75
- input_projection: bfloat16 [1536, 6144], P('fsdp', 'member'), may hold values from -0.15625 to 0.15625
- output_projection: bfloat16 [6144, 1536], P('member', 'fsdp'), may hold values from -0.078125 to 0.078125
- adapter_down_map: bfloat16 [16, 1536, 64], P('member'), may hold values from -0.15625 to 0.15625
- adapter_up_map: bfloat16 [16, 64, 6144], P('member'), may hold values from -0.75 to 0.75
- lengths: int32 [16, 32], P('member', 'fsdp'), may hold values from 90 to 126, as said below
- cotangent: bfloat16 [16, 4608, 1536], P('member', 'fsdp'), may hold values from -0.29882812 to 0.29882812
Outputs:
- down_map_gradient: float32 [16, 1536, 64], P('member')
- up_map_gradient: float32 [16, 64, 6144], P('member')
Inputs may be any that keep to these rules, and one draw needn't show every extreme that they name: `lengths`: each member has at least one utterance of exactly 126 frames.
All inputs are finite; a program needn't handle non-finite values.
Results may differ from a plain program's by a relative error of at most 0.0058.
Values may be sent and summed in bfloat16 or wider, within the bound.
A program may use at most 128 MiB of HBM per device.

v0:
```python
import jax
import jax.numpy as jnp
from jax import lax
from jax.sharding import PartitionSpec as P

BUCKET = 144


def on_device(
    frames,
    layer_norm_gain,
    input_projection,
    output_projection,
    adapter_down_map,
    adapter_up_map,
    lengths,
    cotangent,
):
    members = lax.axis_size("member")
    values = frames[0].astype(jnp.float32)
    mean = jnp.mean(values, axis=1, keepdims=True)
    var = jnp.mean((values - mean) ** 2, axis=1, keepdims=True)
    normed_input = (layer_norm_gain * (values - mean) / jnp.sqrt(var + 1e-05)).astype(jnp.bfloat16)
    low_rank_state = jnp.dot(
        normed_input, adapter_down_map[0], preferred_element_type=jnp.float32
    ).astype(jnp.bfloat16)
    positions = jnp.arange(BUCKET, dtype=jnp.int32)
    mask = (positions[None, :] < lengths[0][:, None]).reshape(-1)
    masked = cotangent[0] * mask.astype(cotangent.dtype)[:, None]
    rows = normed_input.shape[0]
    up_map_slices = lax.all_to_all(
        adapter_up_map, "member", split_axis=2, concat_axis=0, tiled=True
    )
    stacked_norm, stacked_low, stacked_grad = (
        lax.all_gather(normed_input, "member", axis=0, tiled=True),
        lax.all_gather(low_rank_state, "member", axis=0, tiled=True),
        lax.all_gather(masked, "member", axis=0, tiled=True),
    )
    low_rank_blocks = stacked_low.reshape(members, rows, -1)
    adapter_term = jnp.einsum(
        "dgs,dsb->dgb", low_rank_blocks, up_map_slices, preferred_element_type=jnp.float32
    )
    adapter_term = adapter_term.reshape(members * rows, -1)
    columns = stacked_norm
    pre = adapter_term + jnp.dot(
        columns,
        lax.all_gather(input_projection, "fsdp", axis=0, tiled=True),
        preferred_element_type=jnp.float32,
    )
    columns = stacked_grad
    dhid = 0.5 * lax.dot_general(
        columns,
        lax.all_gather(output_projection, "fsdp", axis=1, tiled=True),
        (((1,), (1,)), ((), ())),
        preferred_element_type=jnp.float32,
    )
    sigma = jax.nn.sigmoid(pre)
    dpre = (dhid * sigma * (1.0 + pre * (1.0 - sigma))).astype(jnp.bfloat16)
    preact_gradient_blocks = dpre.reshape(members, rows, -1)
    up_partial = jnp.einsum(
        "jnz,jnv->jzv", low_rank_blocks, preact_gradient_blocks, preferred_element_type=jnp.float32
    )
    back_partial = jnp.einsum(
        "yha,ywa->yhw", preact_gradient_blocks, up_map_slices, preferred_element_type=jnp.float32
    )
    back = lax.psum_scatter(back_partial, "member", scatter_dimension=0, tiled=True)[0].astype(
        jnp.bfloat16
    )
    down_partial = jnp.dot(normed_input.T, back, preferred_element_type=jnp.float32)
    up_summed = lax.psum(up_partial, "fsdp")
    up_map_gradient = lax.all_to_all(up_summed, "member", split_axis=0, concat_axis=2, tiled=True)
    down_map_gradient = lax.psum(down_partial, "fsdp")
    return (down_map_gradient[None], up_map_gradient)


def solution(mesh):
    in_specs = (
        P("member", "fsdp", None),
        P(),
        P("fsdp", "member"),
        P("member", "fsdp"),
        P("member", None, None),
        P("member", None, None),
        P("member", "fsdp"),
        P("member", "fsdp", None),
    )
    out_specs = (P("member", None, None), P("member", None, None))
    return jax.shard_map(
        on_device, mesh=mesh, in_specs=in_specs, out_specs=out_specs, check_vma=False
    )
```

profile of v0, /device:TPU:1, one launch (start us, length us, event | category | flops | bytes accessed | tf_op | source)
XLA Modules:
  0.0 1449.9 jit_solution(2812259246271979070)
XLA Ops:
  7.2 0.0 copy-start
  7.2 0.0 all-gather.12.cloned.1.call-start
  7.2 0.7 all-gather.12.cloned.1.call-update
  7.9 0.0 all-gather.10.cloned.1.call-start
  8.0 1.2 convert_reduce_fusion
  9.1 1.3 fusion.10
  10.4 2.0 fusion.12
  12.4 0.0 all-gather.10.cloned.1.call-update
  12.5 0.0 all-gather.8.cloned.1.call-start
  12.5 0.7 all-gather.8.cloned.1.call-update
  13.2 0.0 all-gather.6.cloned.1.call-start
  13.9 1.9 bitcast_multiply_fusion
  15.8 0.0 all-gather.6.cloned.1.call-update
  15.8 6.7 copy.12
  22.5 0.5 broadcast.58
  23.0 34.4 %reduce.1 = bf16[6144,64]{1,0:T(8,128)(2,1)} reduce(bf16[6144,1,64]{2,1,0:T(2,128)(2,1)S(1)} %bitcast.57, bf16[]{:T(256)} %broadcast.58), dimensions={1}, to_apply=%bitcast.44.reduce_sub_computation | reduce | bytes 1572866
  57.5 3.9 reshape.87
  61.4 19.2 %all-to-all-start = ((bf16[16,2,12288]{2,1,0:T(2,128)(2,1)}), bf16[16,2,12288]{2,1,0:T(2,128)(2,1)}, u32[]{:S(2)}, u32[]{:S(2)}) async-start(bf16[16,2,12288]{2,1,0:T(2,128)(2,1)} %reshape.87), calls=%async_computation | async-start | bytes 1572864 | tf_op jit(solution)/shard_map/all_to_all | solution.py:31
  80.6 0.0 reduce-scatter.2.cloned.1.call-start
  80.7 0.2 fusion.17
  80.9 0.0 copy-start.3
  80.9 0.7 copy-done.3
  81.7 0.3 fusion.3
  81.9 75.8 %all-gather = bf16[16,144,64]{1,2,0:T(8,128)(2,1)} all-gather(bf16[1,144,64]{1,2,0:T(8,128)(2,1)S(1)} %fusion.3), channel_id=1, replica_groups=mesh['fsdp'=32,'member'=16] {'member'}, dimensions={0}, use_global_device_ids=true | all-gather | bytes 313344 | tf_op jit(solution)/shard_map/all_gather | solution.py:36
  157.8 0.0 all-to-all-done
  157.8 4.6 reshape.88
  162.3 1.3 copy.18
  163.7 1.7 copy.14
  165.4 3.5 fusion.15
  168.9 70.4 %all-gather.12.cloned.1.call-done = bf16[1536,384]{1,0:T(8,128)(2,1)} async-done(((bf16[48,384]{1,0:T(8,128)(2,1)}), bf16[1536,384]{1,0:T(8,128)(2,1)}) %all-gather.12.cloned.1.call-update) | async-done | bytes 1179664 | tf_op jit(solution)/shard_map/all_gather | solution.py:47
  239.3 179.4 %all-gather.10.cloned.1.call-done = bf16[2304,1536]{1,0:T(8,128)(2,1)} async-done(((bf16[144,1536]{1,0:T(8,128)(2,1)}), bf16[2304,1536]{1,0:T(8,128)(2,1)}) %all-gather.10.cloned.1.call-update) | async-done | bytes 7077904 | tf_op jit(solution)/shard_map/all_gather | solution.py:35
  418.7 10.0 convolution_add_fusion
  428.7 184.5 %all-gather.8.cloned.1.call-done = bf16[384,1536]{0,1:T(8,128)(2,1)} async-done(((bf16[384,48]{0,1:T(8,128)(2,1)}), bf16[384,1536]{0,1:T(8,128)(2,1)}) %all-gather.8.cloned.1.call-update) | async-done | bytes 1179664 | tf_op jit(solution)/shard_map/all_gather | solution.py:53
  613.2 183.5 %all-gather.6.cloned.1.call-done = bf16[2304,1536]{1,0:T(8,128)(2,1)} async-done(((bf16[144,1536]{1,0:T(8,128)(2,1)}), bf16[2304,1536]{1,0:T(8,128)(2,1)}) %all-gather.6.cloned.1.call-update) | async-done | bytes 7077904 | tf_op jit(solution)/shard_map/all_gather | solution.py:37
  796.6 9.0 fusion.2
  805.6 0.0 copy-start.2
  805.6 1.9 fusion.13
  807.5 0.0 reduce-scatter.2.cloned.1.call-update
  807.5 0.0 all-reduce.3.cloned.1.call-start
  807.6 0.0 copy-done.2
  807.6 1.6 fusion.21
  809.2 94.6 %reduce-scatter.2.cloned.1.call-done = f32[1,144,64]{1,2,0:T(8,128)} async-done(((f32[16,144,64]{1,2,0:T(8,128)}), f32[1,144,64]{1,2,0:T(8,128)}) %reduce-scatter.2.cloned.1.call-update) | async-done | bytes 36880 | tf_op jit(solution)/shard_map/reduce_scatter | solution.py:66
  903.9 1.8 convolution_bitcast_fusion
  905.7 0.0 all-reduce.3.cloned.1.call-update
  905.7 434.8 %all-reduce.3.cloned.1.call-done = (f32[1,1536,64]{1,2,0:T(8,128)}, f32[16,64,384]{2,1,0:T(8,128)}) async-done(((f32[1,1536,64]{1,2,0:T(8,128)}, f32[16,64,384]{2,1,0:T(8,128)}), (f32[1,1536,64]{1,2,0:T(8,128)}, f32[16,64,384]{2,1,0:T(8,128)})) %all-reduce.3.cloned.1.call-update) | async-done | bytes 1966096 | tf_op jit(solution)/shard_map/psum | solution.py:72
  1340.4 100.6 %all_to_all.36 = f32[16,64,384]{2,1,0:T(8,128)S(1)} all-to-all(f32[16,64,384]{2,1,0:T(8,128)} %get-tuple-element.3), channel_id=1, replica_groups=mesh['fsdp'=32,'member'=16] {'member'}, dimensions={0} | all-to-all | bytes 3145728 | tf_op jit(solution)/shard_map/all_to_all | solution.py:71
  1441.0 1.2 copy.19
  1442.3 0.7 copy.23
  (12 shorter events, 0.0 us)
Async XLA Ops:
  7.2 74.5 %copy-start = (bf16[1,1536,64]{1,2,0:T(8,128)(2,1)S(1)}, bf16[1,1536,64]{1,2,0:T(8,128)(2,1)}, u32[]{:S(2)}) copy-start(bf16[1,1536,64]{1,2,0:T(8,128)(2,1)} %param.12) | copy-start | bytes 589828
  7.2 232.1 %all-gather.12.cloned.1.call-start = ((), (), s32[]{:S(2)}) async-start(), calls=%async_computation.6 | async-start | bytes 1216512 | tf_op jit(solution)/shard_map/all_gather | solution.py:47
  7.9 410.8 %all-gather.10.cloned.1.call-start = ((), (), s32[]{:S(2)}) async-start(), calls=%async_computation.5 | async-start | bytes 7520256 | tf_op jit(solution)/shard_map/all_gather | solution.py:35
  12.5 600.7 %all-gather.8.cloned.1.call-start = ((), (), s32[]{:S(2)}) async-start(), calls=%async_computation.4 | async-start | bytes 1216512 | tf_op jit(solution)/shard_map/all_gather | solution.py:53
  13.2 783.4 %all-gather.6.cloned.1.call-start = ((), (), s32[]{:S(2)}) async-start(), calls=%async_computation.3 | async-start | bytes 7520256 | tf_op jit(solution)/shard_map/all_gather | solution.py:37
  23.0 57.6 %copy-start.6 = (f32[1536]{0:T(1024)S(1)}, f32[1536]{0:T(1024)}, u32[]{:S(2)}) copy-start(f32[1536]{0:T(1024)} %param.9) | copy-start | bytes 18436
  57.5 23.2 %copy-start.1 = (bf16[1,144,1536]{2,1,0:T(8,128)(2,1)S(1)}, bf16[1,144,1536]{2,1,0:T(8,128)(2,1)}, u32[]{:S(2)}) copy-start(bf16[1,144,1536]{2,1,0:T(8,128)(2,1)} %param.8) | copy-start | bytes 1327108
  61.4 96.4 %all-to-all-start = ((bf16[16,2,12288]{2,1,0:T(2,128)(2,1)}), bf16[16,2,12288]{2,1,0:T(2,128)(2,1)}, u32[]{:S(2)}, u32[]{:S(2)}) async-start(bf16[16,2,12288]{2,1,0:T(2,128)(2,1)} %reshape.87), calls=%async_computation | async-start | bytes 1572864 | tf_op jit(solution)/shard_map/all_to_all | solution.py:31
  80.6 823.2 %reduce-scatter.2.cloned.1.call-start = ((), (), s32[]{:S(2)}) async-start(), calls=%async_computation.7 | async-start | bytes 1114112 | tf_op jit(solution)/shard_map/reduce_scatter | solution.py:66
  80.9 0.8 copy-start.3
  805.6 2.0 copy-start.2
  807.5 96.3 %copy-start.4 = (bf16[144,1536]{1,0:T(8,128)(2,1)S(1)}, bf16[144,1536]{1,0:T(8,128)(2,1)}, u32[]{:S(2)}) copy-start(bf16[144,1536]{1,0:T(8,128)(2,1)} %copy-done.3) | copy-start | bytes 1327108
  807.5 532.9 %all-reduce.3.cloned.1.call-start = ((), (), s32[]{:S(2)}) async-start(), calls=%async_computation.8 | async-start | bytes 3932160 | tf_op jit(solution)/shard_map/psum | solution.py:72
  1340.4 101.8 %copy-start.5 = (f32[1,1536,64]{1,2,0:T(8,128)S(1)}, f32[1,1536,64]{1,2,0:T(8,128)}, u32[]{:S(2)}) copy-start(f32[1,1536,64]{1,2,0:T(8,128)} %get-tuple-element.4) | copy-start | bytes 1179652
Sparse Core Ops, SparseCore 0:
  10.1 229.1 all-gather.11
  242.5 176.1 all-gather.9
  420.8 192.3 all-gather.7
  616.3 180.3 all-gather.5
  807.7 96.1 reduce-scatter.1
  907.6 432.8 all-reduce.2
where the time goes:
time: 1450 us
  waiting for transfers between devices  1150 us (79%)
  blocking collectives  176 us (12%)
  other arithmetic  41.1 us (3%)
  matrix products  28 us (2%)
  local copies, waits for them, and re-layouts  21.5 us (1%)
  starting transfers between devices  19.5 us (1%)
  between operations  14.9 us (1%)
    psum x1, waiting for transfers between devices, on_device(): down_map_gradient = lax.psum(down_partial, 'fsdp')  435 us
    all_gather x1, waiting for transfers between devices, on_device(): lax.all_gather(output_projection, 'fsdp', axis=1, tiled=True)  184 us
    all_gather x1, waiting for transfers between devices, on_device(): lax.all_gather(masked, 'member', axis=0, tiled=True)  183 us
    all_gather x1, waiting for transfers between devices, on_device(): lax.all_gather(normed_input, 'member', axis=0, tiled=True)  179 us
    all_to_all x1, blocking collectives, on_device(): lax.all_to_all(up_summed, 'member', split_axis=0, concat_axis=2, tiled=True)  101 us
    reduce_scatter x1, waiting for transfers between devices, on_device(): lax.psum_scatter(back_partial, 'member', scatter_dimension=0, tiled=True)[0]  94.6 us
    all_gather x1, blocking collectives, on_device(): lax.all_gather(low_rank_state, 'member', axis=0, tiled=True)  75.8 us
    all_gather x1, waiting for transfers between devices, on_device(): lax.all_gather(input_projection, 'fsdp', axis=0, tiled=True)  70.4 us
  transfers between devices with their start and end apart: 7, of which 6 were waited for; matrix products, arithmetic and copies ran while one was open for 5% of the time, Pallas kernels for 0%

commit v1 on v0

v1 whole, which is shorter than its diff:
```python
import jax
import jax.numpy as jnp
from jax import lax
from jax.experimental import pallas as pl
from jax.experimental.pallas import tpu as pltpu
from jax.sharding import PartitionSpec as P

MESH = pl.DeviceIdType.MESH
ROWS = 128
D = 1536
RANK = 64
LOW = D
COT = D + 128
WIDE = 2 * D + 128
F32 = jnp.float32
BF16 = jnp.bfloat16


def dot(a, b, dims=((1,), (0,))):
    return lax.dot_general(a, b, (dims, ((), ())), preferred_element_type=F32)


def kernel(
    frames, gain, w1, w2, down_map, up_map, lengths, cot,
    dn_out, up_out,
    ws_a, ws_b, wa, wb, tok, ub, bks, bkr, bka, rss, rsr, dns, dnr, ag,
    tp_s, tp_r, tk_s, tk_r, td_s, td_r, u_s, u_r,
    ay_s, ay_r, az_s, az_r, bz_s, bz_r, by_s, by_r, bo_s, bo_r,
    bk_s, bk_r, ba_s, ba_r, rs_s, rs_r, dn_s, dn_r, gz_s, gz_r, gx_s, gx_r,
):
    fi = lax.axis_index("fsdp")
    mi = lax.axis_index("member")
    x, zl = fi // 8, fi % 8
    y, zh, c = mi // 4, (mi // 2) % 2, mi % 2
    z = zh * 8 + zl

    def dev(x_, y_, z_, c_):
        return (x_ * 8 + z_ % 8, y_ * 4 + (z_ // 8) * 2 + c_)

    xr, xl, xo = (x + 1) % 4, (x + 3) % 4, (x + 2) % 4
    yr, yl, yo = (y + 1) % 4, (y + 3) % 4, (y + 2) % 4
    right, left = dev(xr, y, z, c), dev(xl, y, z, c)
    up, dn = dev(x, yr, z, c), dev(x, yl, z, c)
    fore, aft = dev(x, y, (z + 1) % 16, c), dev(x, y, (z + 15) % 16, c)
    twin = dev(x, y, z, 1 - c)
    flip = dev(y, x, z, c)

    def zdev(d, c_):
        return dev(x, y, zh * 8 + (zl + d) % 8, c_)

    def rcopy(src, dst, ss, rs, to):
        return pltpu.make_async_remote_copy(
            src_ref=src, dst_ref=dst, send_sem=ss, recv_sem=rs, device_id=to, device_id_type=MESH
        )

    barrier = pltpu.get_barrier_semaphore()
    peers = [up, dn, fore, aft, twin]
    for d in range(1, 4):
        for c_ in range(2):
            peers.append(dev((x + d) % 4, y, z, c_))
    for d in range(1, 8):
        for c_ in range(2):
            peers.append(zdev(d, c_))
    for peer in peers:
        pl.semaphore_signal(barrier, inc=1, device_id=peer, device_id_type=MESH)

    @pl.when(x != y)
    def _():
        pl.semaphore_signal(barrier, inc=1, device_id=flip, device_id_type=MESH)

    eye = (
        lax.broadcasted_iota(jnp.int32, (48, 48), 0) == lax.broadcasted_iota(jnp.int32, (48, 48), 1)
    ).astype(BF16)
    w2t = dot(eye, w2[...], ((1,), (1,))).astype(BF16)
    ws_a[0] = w1[:, 0:128]
    ws_b[0] = w1[:, 128:384]
    ws_a[1] = w2t[:, 0:128]
    ws_b[1] = w2t[:, 128:384]

    pl.semaphore_wait(barrier, len(peers) + jnp.where(x != y, 1, 0))

    def tp_copies():
        return [
            rcopy(ws_a.at[0], wa.at[zh, x, zl], tp_s.at[0], tp_r.at[0], flip),
            rcopy(ws_a.at[1], wa.at[zh, 4 + x, zl], tp_s.at[1], tp_r.at[1], flip),
            rcopy(ws_b, wb.at[zh, :, x, zl], tp_s.at[2], tp_r.at[2], flip),
        ]

    @pl.when(x != y)
    def _():
        for cp in tp_copies():
            cp.start()

    @pl.when(x == y)
    def _():
        for w in range(2):
            wa[zh, 4 * w + y, zl] = ws_a[w]
            wb[zh, w, y, zl] = ws_b[w]

    v = frames[0, 0:ROWS, :].astype(F32)
    mean = jnp.mean(v, axis=1, keepdims=True)
    var = jnp.mean((v - mean) ** 2, axis=1, keepdims=True)
    normed = (gain[...] * (v - mean) / jnp.sqrt(var + 1e-05)).astype(BF16)
    low = dot(normed, down_map[0]).astype(BF16)
    keep = lax.broadcasted_iota(jnp.int32, (ROWS, D), 0) < lengths[0, 0]
    masked = jnp.where(keep, cot[0, 0:ROWS, :].astype(F32), 0.0).astype(BF16)
    tok[x, c, :, 0:D] = normed
    tok[x, c, :, LOW : LOW + 128] = jnp.concatenate([low, jnp.zeros_like(low)], axis=1)
    tok[x, c, :, COT:WIDE] = masked

    def half(x_, h):
        return tok.at[x_, c, pl.ds(64 * h, 64), :]

    def halfo(x_, h):
        return tok.at[x_, 1 - c, pl.ds(64 * h, 64), :]

    def t_copy(i):
        x_, h, to = [
            (x, 0, right), (x, 1, right), (x, 1, left), (x, 0, left), (xl, 0, right), (xr, 1, left)
        ][i]
        return rcopy(half(x_, h), half(x_, h), tk_s.at[i], tk_r.at[i], to)

    def t_wait(i):
        x_, h = [(xl, 0), (xl, 1), (xr, 1), (xr, 0), (xo, 0), (xo, 1)][i]
        rcopy(half(x_, h), half(x_, h), tk_s.at[i], tk_r.at[i], right).wait_recv()

    def d_copy(r, h):
        x_ = [x, xl, xr, xo][r]
        return rcopy(half(x_, h), half(x_, h), td_s.at[2 * r + h], td_r.at[2 * r + h], twin)

    def d_wait(r, h):
        x_ = [x, xl, xr, xo][r]
        rcopy(halfo(x_, h), halfo(x_, h), td_s.at[2 * r + h], td_r.at[2 * r + h], twin).wait_recv()

    for i in (0, 2, 1, 3):
        t_copy(i).start()

    def a_blk(s):
        z_ = (z + s + 16) % 16
        return wa.at[z_ // 8, :, z_ % 8]

    def a_half(s, w):
        z_ = (z + s + 16) % 16
        return wa.at[z_ // 8, pl.ds(4 * w, 4), z_ % 8]

    def a_one(y_, w):
        return wa.at[zh, 4 * w + y_, zl]

    def b_blk(s, y_):
        z_ = (z + s + 16) % 16
        return wb.at[z_ // 8, :, y_, z_ % 8]

    def b_half(s, y_, w):
        z_ = (z + s + 16) % 16
        return wb.at[z_ // 8, w, y_, z_ % 8]

    def ay_copy(i):
        y_, w, to = [(y, 0, up), (y, 1, up), (y, 0, dn), (y, 1, dn), (yl, 0, up), (yr, 1, dn)][i]
        return rcopy(a_one(y_, w), a_one(y_, w), ay_s.at[i], ay_r.at[i], to)

    def ay_wait(i):
        y_, w = [(yl, 0), (yl, 1), (yr, 0), (yr, 1), (yo, 0), (yo, 1)][i]
        rcopy(a_one(y_, w), a_one(y_, w), ay_s.at[i], ay_r.at[i], up).wait_recv()

    def z_full(route, k, make, ss, rs):
        s = (-(k - 1)) if route == 0 else (k - 1)
        return rcopy(make(s), make(s), ss.at[route, k], rs.at[route, k], fore if route == 0 else aft)

    def z_half(route, make, ss, rs):
        s = -7 if route == 0 else 7
        return rcopy(make(s, route), make(s, route), ss.at[route, 8], rs.at[route, 8], fore if route == 0 else aft)

    def z_wait(route, k, make, ss, rs):
        s = -k if route == 0 else k
        rcopy(make(s), make(s), ss.at[route, k], rs.at[route, k], fore).wait_recv()

    def z_wait_half(route, make, ss, rs):
        rcopy(make(8, route), make(8, route), ss.at[route, 8], rs.at[route, 8], fore).wait_recv()

    def b_own(s):
        return b_blk(s, y)

    def b_own_half(s, w):
        return b_half(s, y, w)

    def by_copy(s, j, way):
        return rcopy(b_blk(s, y), b_blk(s, y), by_s.at[way, j], by_r.at[way, j], up if way == 0 else dn)

    def by_wait(s, j, way):
        y_ = yl if way == 0 else yr
        rcopy(b_blk(s, y_), b_blk(s, y_), by_s.at[way, j], by_r.at[way, j], up).wait_recv()

    def bo_copy(s, j, way):
        y_ = yl if way == 0 else yr
        return rcopy(
            b_half(s, y_, way), b_half(s, y_, way), bo_s.at[way, j], bo_r.at[way, j], up if way == 0 else dn
        )

    def bo_wait(s, j, way):
        rcopy(b_half(s, yo, way), b_half(s, yo, way), bo_s.at[way, j], bo_r.at[way, j], up).wait_recv()

    @pl.when(x != y)
    def _():
        for cp in tp_copies():
            cp.wait_recv()

    for i in range(4):
        ay_copy(i).start()
    for route in range(2):
        z_full(route, 1, b_own, bz_s, bz_r).start()
    for way in range(2):
        by_copy(0, 0, way).start()

    for h in range(2):
        d_copy(0, h).start()

    def u_cols(zh_, c_):
        return up_map.at[0, :, pl.ds(pl.multiple_of(((x * 2 + zh_) * 2 + c_) * 384, 128), 384)]

    def u_local(zh_):
        return pltpu.make_async_copy(u_cols(zh_, c), ub.at[c, zh_], u_s.at[2 + zh_])

    def u_copy(zh_):
        return rcopy(u_cols(zh_, 1 - c), ub.at[c, zh_], u_s.at[zh_], u_r.at[zh_], twin)

    for zh_ in range(2):
        u_local(zh_).start()
        u_copy(zh_).start()

    ay_wait(0)
    ay_copy(4).start()
    ay_wait(3)
    ay_copy(5).start()
    for i in (1, 2, 4, 5):
        ay_wait(i)
    for route in range(2):
        z_full(route, 1, a_blk, az_s, az_r).start()

    def y_stage(s, j):
        for way in range(2):
            by_wait(s, j, way)
            bo_copy(s, j, way).start()

    def step(k, _):
        for route in range(2):
            z_wait(route, k, b_own, bz_s, bz_r)
            z_full(route, k + 1, b_own, bz_s, bz_r).start()
            s = -k if route == 0 else k
            for way in range(2):
                by_copy(s, 2 * k - 1 + route, way).start()
        for route in range(2):
            z_wait(route, k, a_blk, az_s, az_r)
            z_full(route, k + 1, a_blk, az_s, az_r).start()
        for route in range(2):
            s = -(k - 1) if route == 0 else (k - 1)

            @pl.when((k > 1) | (route == 0))
            def _():
                y_stage(s, jnp.where(k == 1, 0, 2 * k - 3 + route))
        return 0

    lax.fori_loop(1, 4, step, 0)
    t_wait(0)
    t_copy(4).start()
    d_copy(1, 0).start()
    t_wait(2)
    t_copy(5).start()
    d_copy(2, 1).start()
    lax.fori_loop(4, 7, step, 0)
    t_wait(1)
    d_copy(1, 1).start()
    t_wait(3)
    d_copy(2, 0).start()
    for route in range(2):
        z_wait(route, 7, b_own, bz_s, bz_r)
        z_half(route, b_own_half, bz_s, bz_r).start()
        s = -7 if route == 0 else 7
        for way in range(2):
            by_copy(s, 13 + route, way).start()
    for route in range(2):
        z_wait(route, 7, a_blk, az_s, az_r)
        z_half(route, a_half, az_s, az_r).start()
    y_stage(-6, 11)
    y_stage(6, 12)
    for route in range(2):
        z_wait_half(route, b_own_half, bz_s, bz_r)
    for way in range(2):
        by_copy(8, 15, way).start()
    for route in range(2):
        z_wait_half(route, a_half, az_s, az_r)
    y_stage(-7, 13)
    y_stage(7, 14)
    for i in (4, 5):
        t_wait(i)
        d_copy(3, i - 4).start()
    y_stage(8, 15)

    def bo_step(j, _):
        s = jnp.where(j % 2 == 1, -((j + 1) // 2), (j + 1) // 2)
        for way in range(2):
            bo_wait(s, j, way)
        return 0

    for way in range(2):
        bo_wait(0, 0, way)
    lax.fori_loop(1, 15, bo_step, 0)
    for way in range(2):
        bo_wait(8, 15, way)
    for r in range(4):
        for h in range(2):
            d_wait(r, h)
    for zh_ in range(2):
        u_local(zh_).wait()
        rcopy(ub.at[1 - c, zh_], ub.at[1 - c, zh_], u_s.at[zh_], u_r.at[zh_], twin).wait_recv()

    def member(m, _):
        lo = tok[:, m, :, LOW : LOW + 128].reshape(4 * ROWS, 128)
        for b in range(4):
            zh_, is_b = b // 2, b % 2
            c0, c1 = (128, 384) if is_b else (0, 128)
            if is_b:
                wi, wo = wb[zh_, 0].reshape(D, 256), wb[zh_, 1].reshape(D, 256)
            else:
                wi, wo = wa[zh_, 0:4].reshape(D, 128), wa[zh_, 4:8].reshape(D, 128)
            u = ub[m, zh_, :, c0:c1]
            pre = dot(tok[:, m, :, 0:D].reshape(4 * ROWS, D), wi) + dot(lo[:, 0:RANK], u)
            dhid = 0.5 * dot(tok[:, m, :, COT:WIDE].reshape(4 * ROWS, D), wo)
            sig = jax.nn.sigmoid(pre)
            dpre = (dhid * sig * (1.0 + pre * (1.0 - sig))).astype(BF16)
            part = dot(lo, dpre, ((0,), (0,)))
            for r in range(8):
                rss[m, r, :, zh_ * 384 + c0 : zh_ * 384 + c1] = part[8 * r : 8 * r + 8].astype(BF16)
            for x_ in range(4):
                bp = dot(u, dpre[ROWS * x_ : ROWS * (x_ + 1)], ((1,), (1,)))
                if b == 0:
                    bks[x_, m] = bp
                else:
                    bks[x_, m] += bp
        return 0

    lax.fori_loop(0, 2, member, 0)

    def bk_copy(d, c_):
        x_ = (x + d) % 4
        return rcopy(bks.at[x_, c_], bkr.at[x, c], bk_s.at[d, c_], bk_r.at[d, c], dev(x_, y, z, c_))

    def bk_other():
        return rcopy(bks.at[x, 1 - c], bkr.at[x, c], bk_s.at[0, 0], bk_r.at[0, 0], twin)

    bk_other().start()
    for d in range(1, 4):
        for c_ in range(2):
            bk_copy(d, c_).start()

    def rs_copy(d, c_):
        return rcopy(rss.at[c_, (zl + d) % 8], rsr.at[zl, c], rs_s.at[d, c_], rs_r.at[d, c], zdev(d, c_))

    def rs_other():
        return rcopy(rss.at[1 - c, zl], rsr.at[zl, c], rs_s.at[0, 0], rs_r.at[0, 0], twin)

    rs_other().start()
    for d in range(1, 8):
        for c_ in range(2):
            rs_copy(d, c_).start()
    rsr[zl, c] = rss[c, zl]
    bkr[x, c] = bks[x, c]

    rcopy(bkr.at[x, 1 - c], bkr.at[x, 1 - c], bk_s.at[0, 0], bk_r.at[0, 0], twin).wait_recv()
    for d in range(1, 4):
        for c_ in range(2):
            slot = bkr.at[(x + 4 - d) % 4, c_]
            rcopy(slot, slot, bk_s.at[d, c_], bk_r.at[d, c_], twin).wait_recv()
    total = bkr[0, 0]
    for i in range(1, 8):
        total = total + bkr[i // 2, i % 2]
    bka[x] = total.astype(BF16)

    def ba_copy(d):
        return rcopy(bka.at[x], bka.at[x], ba_s.at[d], ba_r.at[d], dev((x + d) % 4, y, z, c))

    for d in range(1, 4):
        ba_copy(d).start()
    for d in range(1, 4):
        slot = bka.at[(x + 4 - d) % 4]
        rcopy(slot, slot, ba_s.at[d], ba_r.at[d], right).wait_recv()
    quarter = pl.ds(pl.multiple_of(x * 384, 128), 384)
    part = dot(bka[0], tok[0, c, :, quarter])
    for x_ in range(1, 4):
        part = part + dot(bka[x_], tok[x_, c, :, quarter])
    for r in range(8):
        dns[r] = part[8 * r : 8 * r + 8].astype(BF16)

    def dn_copy(d):
        return rcopy(dns.at[(zl + d) % 8], dnr.at[zl], dn_s.at[d], dn_r.at[d], zdev(d, c))

    for d in range(1, 8):
        dn_copy(d).start()
    dnr[zl] = dns[zl]

    other = rsr.at[zl, 1 - c]
    rcopy(other, other, rs_s.at[0, 0], rs_r.at[0, 0], twin).wait_recv()
    for d in range(1, 8):
        for c_ in range(2):
            slot = rsr.at[(zl + 8 - d) % 8, c_]
            rcopy(slot, slot, rs_s.at[d, c_], rs_r.at[d, c_], twin).wait_recv()
    for c_ in range(2):
        total = rsr[0, c_].astype(F32)
        for i in range(1, 8):
            total = total + rsr[i, c_].astype(F32)
        ag[x, zl, :, 768 * c_ : 768 * (c_ + 1)] = total.astype(BF16)
    for d in range(1, 8):
        slot = dnr.at[(zl + 8 - d) % 8]
        rcopy(slot, slot, dn_s.at[d], dn_r.at[d], twin).wait_recv()
    total = dnr[0].astype(F32)
    for i in range(1, 8):
        total = total + dnr[i].astype(F32)
    ag[x, zl, :, 1536:1920] = total.astype(BF16)

    def gz_copy(d):
        return rcopy(ag.at[x, zl], ag.at[x, zl], gz_s.at[d], gz_r.at[d], zdev(d, c))

    for d in range(1, 8):
        gz_copy(d).start()
    for d in range(1, 8):
        slot = ag.at[x, (zl + 8 - d) % 8]
        rcopy(slot, slot, gz_s.at[d], gz_r.at[d], right).wait_recv()

    def g_half(x_, h):
        return ag.at[x_, pl.ds(4 * h, 4)]

    def gx_copy(i):
        x_, h, to = [
            (x, 0, right), (x, 1, right), (x, 1, left), (x, 0, left), (xl, 0, right), (xr, 1, left)
        ][i]
        return rcopy(g_half(x_, h), g_half(x_, h), gx_s.at[i], gx_r.at[i], to)

    def gx_wait(i):
        x_, h = [(xl, 0), (xl, 1), (xr, 1), (xr, 0), (xo, 0), (xo, 1)][i]
        rcopy(g_half(x_, h), g_half(x_, h), gx_s.at[i], gx_r.at[i], right).wait_recv()

    for i in (0, 2, 1, 3):
        gx_copy(i).start()
    gx_wait(0)
    gx_copy(4).start()
    gx_wait(2)
    gx_copy(5).start()
    for i in (1, 3, 4, 5):
        gx_wait(i)

    def write(i, _):
        rows = pl.ds(pl.multiple_of(8 * i, 8), 8)
        for x_ in range(4):
            for c_ in range(2):
                for h in range(2):
                    col = ((x_ * 2 + h) * 2 + c_) * 384
                    src = 768 * c_ + 384 * h
                    up_out[rows, col : col + 384] = ag[x_, i, :, src : src + 384].astype(F32)
            dn_out[rows, 384 * x_ : 384 * (x_ + 1)] = ag[x_, i, :, 1536:1920].astype(F32)
        return 0

    lax.fori_loop(0, 8, write, 0)

    @pl.when(x != y)
    def _():
        for cp in tp_copies():
            cp.wait_send()

    for i in range(6):
        t_copy(i).wait_send()
        ay_copy(i).wait_send()
        gx_copy(i).wait_send()
    for r in range(4):
        for h in range(2):
            d_copy(r, h).wait_send()
    for zh_ in range(2):
        u_copy(zh_).wait_send()
    for route in range(2):
        def z_sent(k, _):
            z_full(route, k, b_own, bz_s, bz_r).wait_send()
            z_full(route, k, a_blk, az_s, az_r).wait_send()
            return 0

        lax.fori_loop(1, 8, z_sent, 0)
        z_half(route, b_own_half, bz_s, bz_r).wait_send()
        z_half(route, a_half, az_s, az_r).wait_send()

        def y_sent(j, _):
            by_copy(0, j, route).wait_send()
            bo_copy(0, j, route).wait_send()
            return 0

        lax.fori_loop(0, 16, y_sent, 0)
    bk_other().wait_send()
    rs_other().wait_send()
    for c_ in range(2):
        for d in range(1, 4):
            bk_copy(d, c_).wait_send()
        for d in range(1, 8):
            rs_copy(d, c_).wait_send()
    for d in range(1, 4):
        ba_copy(d).wait_send()
    for d in range(1, 8):
        dn_copy(d).wait_send()
        gz_copy(d).wait_send()


def on_device(frames, gain, w1, w2, down_map, up_map, lengths, cot):
    vmem = pl.BlockSpec(memory_space=pltpu.VMEM)
    dma = pltpu.SemaphoreType.DMA
    dn, up = pl.pallas_call(
        kernel,
        out_shape=(
            jax.ShapeDtypeStruct((RANK, D), F32),
            jax.ShapeDtypeStruct((RANK, 6144), F32),
        ),
        in_specs=[vmem, vmem, vmem, vmem, vmem, pl.BlockSpec(memory_space=pl.ANY),
                  pl.BlockSpec(memory_space=pltpu.SMEM), vmem],
        out_specs=(vmem, vmem),
        scratch_shapes=[
            pltpu.VMEM((2, 48, 128), BF16),
            pltpu.VMEM((2, 48, 256), BF16),
            pltpu.VMEM((2, 8, 8, 48, 128), BF16),
            pltpu.VMEM((2, 2, 4, 8, 48, 256), BF16),
            pltpu.VMEM((4, 2, ROWS, WIDE), BF16),
            pltpu.VMEM((2, 2, RANK, 384), BF16),
            pltpu.VMEM((4, 2, RANK, ROWS), F32),
            pltpu.VMEM((4, 2, RANK, ROWS), F32),
            pltpu.VMEM((4, RANK, ROWS), BF16),
            pltpu.VMEM((2, 8, 8, 768), BF16),
            pltpu.VMEM((8, 2, 8, 768), BF16),
            pltpu.VMEM((8, 8, 384), BF16),
            pltpu.VMEM((8, 8, 384), BF16),
            pltpu.VMEM((4, 8, 8, 1920), BF16),
            dma((3,)), dma((3,)), dma((6,)), dma((6,)), dma((8,)), dma((8,)), dma((4,)), dma((2,)),
            dma((6,)), dma((6,)), dma((2, 9)), dma((2, 9)), dma((2, 9)), dma((2, 9)),
            dma((2, 16)), dma((2, 16)), dma((2, 16)), dma((2, 16)),
            dma((4, 2)), dma((4, 2)), dma((4,)), dma((4,)), dma((8, 2)), dma((8, 2)),
            dma((8,)), dma((8,)), dma((8,)), dma((8,)), dma((6,)), dma((6,)),
        ],
        compiler_params=pltpu.CompilerParams(
            collective_id=0, has_side_effects=True, vmem_limit_bytes=56 * 1024 * 1024
        ),
    )(frames, gain.reshape(1, D), w1, w2, down_map, up_map, lengths, cot)
    return dn.T[None], up[None]


def solution(mesh):
    in_specs = (
        P("member", "fsdp", None),
        P(),
        P("fsdp", "member"),
        P("member", "fsdp"),
        P("member", None, None),
        P("member", None, None),
        P("member", "fsdp"),
        P("member", "fsdp", None),
    )
    out_specs = (P("member", None, None), P("member", None, None))
    return jax.shard_map(
        on_device, mesh=mesh, in_specs=in_specs, out_specs=out_specs, check_vma=False
    )
```

time: 1450 us -> 126 us (0.09)
  the two profiles are of different devices: /device:TPU:1 before, /device:TPU:32 now
where the time goes in v1:
time: 126 us; the launch traced here: 125 us
  Pallas kernels  115 us (91%)
  local copies, waits for them, and re-layouts  9.08 us (7%)
  between operations  1.29 us (1%)
    pallas_call x1, Pallas kernels, on_device(): pl.pallas_call(kernel, out_shape=(jax.ShapeDtypeStruct((RANK, D), F32), j...  115 us
    unnamed x4, local copies, waits for them, and re-layouts  7.79 us

profile of v1, /device:TPU:32, one launch (start us, length us, event | category | flops | bytes accessed | tf_op | source)
XLA Modules:
  0.0 125.2 jit_solution(957283925221074650)
XLA Ops:
  1.3 1.3 %reshape.7.gain = f32[1,1536]{1,0:T(1,128)} reshape(f32[1536]{0:T(1024)} %param.9) | data formatting | bytes 12288 | tf_op jit(solution)/shard_map/reshape | solution.py:543
  2.6 1.5 %copy.10.w2 = bf16[384,48]{1,0:T(8,128)(2,1)} copy(bf16[384,48]{0,1:T(8,128)(2,1)} %param.11) | data formatting | bytes 73728 | tf_op args[3]
  4.1 1.8 %copy.11.down_map = bf16[1,1536,64]{2,1,0:T(8,128)(2,1)} copy(bf16[1,1536,64]{1,2,0:T(8,128)(2,1)} %param.12) | data formatting | bytes 393216 | tf_op args[4]
  5.9 114.8 %shard_map.95 = (f32[64,1536]{1,0:T(8,128)}, f32[64,6144]{1,0:T(8,128)}) custom-call(bf16[1,144,1536]{2,1,0:T(8,128)(2,1)} %frames.1, f32[1,1536]{1,0:T(1,128)} %reshape.7.gain, bf16[48,384]{1,0:T(8,128)(2,1)} %w1.1, bf16[384,48]{1,0:T(8,128)(2,1)} %copy.10.w2, bf16[1,1536,64]{2,1,0:T(8,128)(2,1)} %copy.11.down_map, bf16[1,64,6144]{2,1,0:T(8,128)(2,1)} %up_map.1, ...), custom_call_target="tpu_custom_call" | custom-call | tf_op jit(solution)/shard_map/pallas_call | solution.py:510
  120.8 1.8 %copy.15 = f32[1,1536,64]{1,2,0:T(8,128)} copy(f32[1,1536,64]{1,2,0:T(8,128)} %bitcast.5) | data formatting | bytes 786432
  122.5 2.7 %copy.16 = f32[1,64,6144]{2,1,0:T(8,128)} copy(f32[1,64,6144]{2,1,0:T(8,128)} %bitcast.4) | data formatting | bytes 3145728

commit v2 on v1

--- a/solution.py
+++ b/solution.py
@@ -21,11 +21,11 @@
 
 
 def kernel(
-    frames, gain, w1, w2, down_map, up_map, lengths, cot,
-    dn_out, up_out,
-    ws_a, ws_b, wa, wb, tok, ub, bks, bkr, bka, rss, rsr, dns, dnr, ag,
-    tp_s, tp_r, tk_s, tk_r, td_s, td_r, u_s, u_r,
-    ay_s, ay_r, az_s, az_r, bz_s, bz_r, by_s, by_r, bo_s, bo_r,
+    frames, gain, w1, w2t, down_map, up_map, lengths, cot,
+    ag,
+    ws_a, ws_b, wa, wb, tok, ub, bks, bkr, bka, rss, rsr, dns, dnr,
+    ta_s, ta_r, tb_s, tb_r, tk_s, tk_r, td_s, td_r, u_s, u_r,
+    az_s, az_r, bz_s, bz_r, by_s, by_r, bo_s, bo_r,
     bk_s, bk_r, ba_s, ba_r, rs_s, rs_r, dn_s, dn_r, gz_s, gz_r, gx_s, gx_r,
 ):
     fi = lax.axis_index("fsdp")
@@ -54,7 +54,7 @@
         )
 
     barrier = pltpu.get_barrier_semaphore()
-    peers = [up, dn, fore, aft, twin]
+    peers = [up, dn, dev(x, yo, z, c), fore, aft, twin]
     for d in range(1, 4):
         for c_ in range(2):
             peers.append(dev((x + d) % 4, y, z, c_))
@@ -64,44 +64,52 @@
     for peer in peers:
         pl.semaphore_signal(barrier, inc=1, device_id=peer, device_id_type=MESH)
 
+    for e in range(1, 4):
+        for peer in (dev((x + e) % 4, x, z, c),):
+            pl.semaphore_signal(barrier, inc=1, device_id=peer, device_id_type=MESH)
+
     @pl.when(x != y)
     def _():
+        pl.semaphore_signal(barrier, inc=1, device_id=dev(x, x, z, c), device_id_type=MESH)
         pl.semaphore_signal(barrier, inc=1, device_id=flip, device_id_type=MESH)
 
-    eye = (
-        lax.broadcasted_iota(jnp.int32, (48, 48), 0) == lax.broadcasted_iota(jnp.int32, (48, 48), 1)
-    ).astype(BF16)
-    w2t = dot(eye, w2[...], ((1,), (1,))).astype(BF16)
     ws_a[0] = w1[:, 0:128]
     ws_b[0] = w1[:, 128:384]
     ws_a[1] = w2t[:, 0:128]
     ws_b[1] = w2t[:, 128:384]
 
-    pl.semaphore_wait(barrier, len(peers) + jnp.where(x != y, 1, 0))
-
-    def tp_copies():
-        return [
-            rcopy(ws_a.at[0], wa.at[zh, x, zl], tp_s.at[0], tp_r.at[0], flip),
-            rcopy(ws_a.at[1], wa.at[zh, 4 + x, zl], tp_s.at[1], tp_r.at[1], flip),
-            rcopy(ws_b, wb.at[zh, :, x, zl], tp_s.at[2], tp_r.at[2], flip),
-        ]
+    pl.semaphore_wait(barrier, len(peers) + jnp.where(x != y, 5, 3))
+
+    def ta_copy(e):
+        to = dev(y, (y + e) % 4, z, c)
+        return rcopy(ws_a, wa.at[zh, :, x, zl], ta_s.at[e], ta_r.at[x], to)
+
+    def ta_wait(a):
+        slot = wa.at[zh, :, a, zl]
+        rcopy(slot, slot, ta_s.at[0], ta_r.at[a], flip).wait_recv()
+
+    def tb_copy():
+        return rcopy(ws_b, wb.at[zh, :, x, zl], tb_s.at[0], tb_r.at[0], flip)
 
     @pl.when(x != y)
     def _():
-        for cp in tp_copies():
-            cp.start()
+        tb_copy().start()
+        ta_copy(0).start()
 
     @pl.when(x == y)
     def _():
         for w in range(2):
-            wa[zh, 4 * w + y, zl] = ws_a[w]
+            wa[zh, w, y, zl] = ws_a[w]
             wb[zh, w, y, zl] = ws_b[w]
+
+    for e in range(1, 4):
+        ta_copy(e).start()
 
     v = frames[0, 0:ROWS, :].astype(F32)
     mean = jnp.mean(v, axis=1, keepdims=True)
     var = jnp.mean((v - mean) ** 2, axis=1, keepdims=True)
-    normed = (gain[...] * (v - mean) / jnp.sqrt(var + 1e-05)).astype(BF16)
-    low = dot(normed, down_map[0]).astype(BF16)
+    normed = (gain[...][None, :] * (v - mean) / jnp.sqrt(var + 1e-05)).astype(BF16)
+    low = dot(normed, down_map[...], ((1,), (1,))).astype(BF16)
     keep = lax.broadcasted_iota(jnp.int32, (ROWS, D), 0) < lengths[0, 0]
     masked = jnp.where(keep, cot[0, 0:ROWS, :].astype(F32), 0.0).astype(BF16)
     tok[x, c, :, 0:D] = normed
@@ -135,16 +143,12 @@
     for i in (0, 2, 1, 3):
         t_copy(i).start()
 
-    def a_blk(s):
+    def a_str(s, w):
         z_ = (z + s + 16) % 16
-        return wa.at[z_ // 8, :, z_ % 8]
-
-    def a_half(s, w):
-        z_ = (z + s + 16) % 16
-        return wa.at[z_ // 8, pl.ds(4 * w, 4), z_ % 8]
-
-    def a_one(y_, w):
-        return wa.at[zh, 4 * w + y_, zl]
+        return wa.at[z_ // 8, w, :, z_ % 8]
+
+    def b_str(s, w):
+        return b_half(s, y, w)
 
     def b_blk(s, y_):
         z_ = (z + s + 16) % 16
@@ -154,34 +158,17 @@
         z_ = (z + s + 16) % 16
         return wb.at[z_ // 8, w, y_, z_ % 8]
 
-    def ay_copy(i):
-        y_, w, to = [(y, 0, up), (y, 1, up), (y, 0, dn), (y, 1, dn), (yl, 0, up), (yr, 1, dn)][i]
-        return rcopy(a_one(y_, w), a_one(y_, w), ay_s.at[i], ay_r.at[i], to)
-
-    def ay_wait(i):
-        y_, w = [(yl, 0), (yl, 1), (yr, 0), (yr, 1), (yo, 0), (yo, 1)][i]
-        rcopy(a_one(y_, w), a_one(y_, w), ay_s.at[i], ay_r.at[i], up).wait_recv()
-
-    def z_full(route, k, make, ss, rs):
-        s = (-(k - 1)) if route == 0 else (k - 1)
-        return rcopy(make(s), make(s), ss.at[route, k], rs.at[route, k], fore if route == 0 else aft)
-
-    def z_half(route, make, ss, rs):
-        s = -7 if route == 0 else 7
-        return rcopy(make(s, route), make(s, route), ss.at[route, 8], rs.at[route, 8], fore if route == 0 else aft)
-
-    def z_wait(route, k, make, ss, rs):
-        s = -k if route == 0 else k
-        rcopy(make(s), make(s), ss.at[route, k], rs.at[route, k], fore).wait_recv()
-
-    def z_wait_half(route, make, ss, rs):
-        rcopy(make(8, route), make(8, route), ss.at[route, 8], rs.at[route, 8], fore).wait_recv()
-
-    def b_own(s):
-        return b_blk(s, y)
-
-    def b_own_half(s, w):
-        return b_half(s, y, w)
+    streams = [(b_str, bz_s, bz_r), (a_str, az_s, az_r)]
+
+    def z_copy(i, w, route, k):
+        make, ss, rs = streams[i]
+        blk = make((-(k - 1)) if route == 0 else (k - 1), w)
+        return rcopy(blk, blk, ss.at[route, w, k], rs.at[route, w, k], fore if route == 0 else aft)
+
+    def z_wait(i, w, route, k):
+        make, ss, rs = streams[i]
+        blk = make(-k if route == 0 else k, w)
+        rcopy(blk, blk, ss.at[route, w, k], rs.at[route, w, k], fore).wait_recv()
 
     def by_copy(s, j, way):
         return rcopy(b_blk(s, y), b_blk(s, y), by_s.at[way, j], by_r.at[way, j], up if way == 0 else dn)
@@ -189,6 +176,14 @@
     def by_wait(s, j, way):
         y_ = yl if way == 0 else yr
         rcopy(b_blk(s, y_), b_blk(s, y_), by_s.at[way, j], by_r.at[way, j], up).wait_recv()
+
+    def by_last(way):
+        blk = b_blk(8, y)
+        return rcopy(blk, blk, by_s.at[way, 15], by_r.at[way, 15], [up, dn, dev(x, yo, z, c)][way])
+
+    def by_last_wait(way):
+        blk = b_blk(8, [yl, yr, yo][way])
+        rcopy(blk, blk, by_s.at[way, 15], by_r.at[way, 15], up).wait_recv()
 
     def bo_copy(s, j, way):
         y_ = yl if way == 0 else yr
@@ -201,15 +196,24 @@
 
     @pl.when(x != y)
     def _():
-        for cp in tp_copies():
-            cp.wait_recv()
-
-    for i in range(4):
-        ay_copy(i).start()
-    for route in range(2):
-        z_full(route, 1, b_own, bz_s, bz_r).start()
+        blk = wb.at[zh, :, y, zl]
+        rcopy(blk, blk, tb_s.at[0], tb_r.at[0], flip).wait_recv()
+
+    for w in range(2):
+        for route in range(2):
+            z_copy(0, w, route, 1).start()
     for way in range(2):
         by_copy(0, 0, way).start()
+    for e in range(1, 4):
+        ta_wait((x + e) % 4)
+
+    @pl.when(x != y)
+    def _():
+        ta_wait(x)
+
+    for w in range(2):
+        for route in range(2):
+            z_copy(1, w, route, 1).start()
 
     for h in range(2):
         d_copy(0, h).start()
@@ -226,15 +230,6 @@
     for zh_ in range(2):
         u_local(zh_).start()
         u_copy(zh_).start()
-
-    ay_wait(0)
-    ay_copy(4).start()
-    ay_wait(3)
-    ay_copy(5).start()
-    for i in (1, 2, 4, 5):
-        ay_wait(i)
-    for route in range(2):
-        z_full(route, 1, a_blk, az_s, az_r).start()
 
     def y_stage(s, j):
         for way in range(2):
@@ -242,15 +237,17 @@
             bo_copy(s, j, way).start()
 
     def step(k, _):
+        for w in range(2):
+            for route in range(2):
+                z_wait(0, w, route, k)
+                z_copy(0, w, route, k + 1).start()
         for route in range(2):
-            z_wait(route, k, b_own, bz_s, bz_r)
-            z_full(route, k + 1, b_own, bz_s, bz_r).start()
-            s = -k if route == 0 else k
             for way in range(2):
-                by_copy(s, 2 * k - 1 + route, way).start()
-        for route in range(2):
-            z_wait(route, k, a_blk, az_s, az_r)
-            z_full(route, k + 1, a_blk, az_s, az_r).start()
+                by_copy(-k if route == 0 else k, 2 * k - 1 + route, way).start()
+        for w in range(2):
+            for route in range(2):
+                z_wait(1, w, route, k)
+                z_copy(1, w, route, k + 1).start()
         for route in range(2):
             s = -(k - 1) if route == 0 else (k - 1)
 
@@ -271,29 +268,34 @@
     d_copy(1, 1).start()
     t_wait(3)
     d_copy(2, 0).start()
+    for w in range(2):
+        for route in range(2):
+            z_wait(0, w, route, 7)
+            if route == w:
+                z_copy(0, w, route, 8).start()
     for route in range(2):
-        z_wait(route, 7, b_own, bz_s, bz_r)
-        z_half(route, b_own_half, bz_s, bz_r).start()
-        s = -7 if route == 0 else 7
         for way in range(2):
-            by_copy(s, 13 + route, way).start()
-    for route in range(2):
-        z_wait(route, 7, a_blk, az_s, az_r)
-        z_half(route, a_half, az_s, az_r).start()
+            by_copy(-7 if route == 0 else 7, 13 + route, way).start()
+    for w in range(2):
+        for route in range(2):
+            z_wait(1, w, route, 7)
+            if route == w:
+                z_copy(1, w, route, 8).start()
     y_stage(-6, 11)
     y_stage(6, 12)
-    for route in range(2):
-        z_wait_half(route, b_own_half, bz_s, bz_r)
-    for way in range(2):
-        by_copy(8, 15, way).start()
-    for route in range(2):
-        z_wait_half(route, a_half, az_s, az_r)
+    for w in range(2):
+        z_wait(0, w, w, 8)
+    for way in range(3):
+        by_last(way).start()
     y_stage(-7, 13)
     y_stage(7, 14)
     for i in (4, 5):
         t_wait(i)
         d_copy(3, i - 4).start()
-    y_stage(8, 15)
+    for w in range(2):
+        z_wait(1, w, w, 8)
+    for way in range(3):
+        by_last_wait(way)
 
     def bo_step(j, _):
         s = jnp.where(j % 2 == 1, -((j + 1) // 2), (j + 1) // 2)
@@ -304,8 +306,6 @@
     for way in range(2):
         bo_wait(0, 0, way)
     lax.fori_loop(1, 15, bo_step, 0)
-    for way in range(2):
-        bo_wait(8, 15, way)
     for r in range(4):
         for h in range(2):
             d_wait(r, h)
@@ -321,7 +321,7 @@
             if is_b:
                 wi, wo = wb[zh_, 0].reshape(D, 256), wb[zh_, 1].reshape(D, 256)
             else:
-                wi, wo = wa[zh_, 0:4].reshape(D, 128), wa[zh_, 4:8].reshape(D, 128)
+                wi, wo = wa[zh_, 0].reshape(D, 128), wa[zh_, 1].reshape(D, 128)
             u = ub[m, zh_, :, c0:c1]
             pre = dot(tok[:, m, :, 0:D].reshape(4 * ROWS, D), wi) + dot(lo[:, 0:RANK], u)
             dhid = 0.5 * dot(tok[:, m, :, COT:WIDE].reshape(4 * ROWS, D), wo)
@@ -447,6 +447,55 @@
     for i in (1, 3, 4, 5):
         gx_wait(i)
 
+    @pl.when(x != y)
+    def _():
+        tb_copy().wait_send()
+        ta_copy(0).wait_send()
+
+    for e in range(1, 4):
+        ta_copy(e).wait_send()
+    for i in range(6):
+        t_copy(i).wait_send()
+        gx_copy(i).wait_send()
+    for r in range(4):
+        for h in range(2):
+            d_copy(r, h).wait_send()
+    for zh_ in range(2):
+        u_copy(zh_).wait_send()
+    for route in range(2):
+        def z_sent(k, _):
+            for w in range(2):
+                for i in range(2):
+                    z_copy(i, w, route, k).wait_send()
+            return 0
+
+        lax.fori_loop(1, 8, z_sent, 0)
+        for i in range(2):
+            z_copy(i, route, route, 8).wait_send()
+
+        def y_sent(j, _):
+            by_copy(0, j, route).wait_send()
+            bo_copy(0, j, route).wait_send()
+            return 0
+
+        lax.fori_loop(0, 15, y_sent, 0)
+    for way in range(3):
+        by_last(way).wait_send()
+    bk_other().wait_send()
+    rs_other().wait_send()
+    for c_ in range(2):
+        for d in range(1, 4):
+            bk_copy(d, c_).wait_send()
+        for d in range(1, 8):
+            rs_copy(d, c_).wait_send()
+    for d in range(1, 4):
+        ba_copy(d).wait_send()
+    for d in range(1, 8):
+        dn_copy(d).wait_send()
+        gz_copy(d).wait_send()
+
+
+def spread(ag, dn_out, up_out):
     def write(i, _):
         rows = pl.ds(pl.multiple_of(8 * i, 8), 8)
         for x_ in range(4):
@@ -460,66 +509,20 @@
 
     lax.fori_loop(0, 8, write, 0)
 
-    @pl.when(x != y)
-    def _():
-        for cp in tp_copies():
-            cp.wait_send()
-
-    for i in range(6):
-        t_copy(i).wait_send()
-        ay_copy(i).wait_send()
-        gx_copy(i).wait_send()
-    for r in range(4):
-        for h in range(2):
-            d_copy(r, h).wait_send()
-    for zh_ in range(2):
-        u_copy(zh_).wait_send()
-    for route in range(2):
-        def z_sent(k, _):
-            z_full(route, k, b_own, bz_s, bz_r).wait_send()
-            z_full(route, k, a_blk, az_s, az_r).wait_send()
-            return 0
-
-        lax.fori_loop(1, 8, z_sent, 0)
-        z_half(route, b_own_half, bz_s, bz_r).wait_send()
-        z_half(route, a_half, az_s, az_r).wait_send()
-
-        def y_sent(j, _):
-            by_copy(0, j, route).wait_send()
-            bo_copy(0, j, route).wait_send()
-            return 0
-
-        lax.fori_loop(0, 16, y_sent, 0)
-    bk_other().wait_send()
-    rs_other().wait_send()
-    for c_ in range(2):
-        for d in range(1, 4):
-            bk_copy(d, c_).wait_send()
-        for d in range(1, 8):
-            rs_copy(d, c_).wait_send()
-    for d in range(1, 4):
-        ba_copy(d).wait_send()
-    for d in range(1, 8):
-        dn_copy(d).wait_send()
-        gz_copy(d).wait_send()
-
 
 def on_device(frames, gain, w1, w2, down_map, up_map, lengths, cot):
     vmem = pl.BlockSpec(memory_space=pltpu.VMEM)
     dma = pltpu.SemaphoreType.DMA
-    dn, up = pl.pallas_call(
+    pieces = pl.pallas_call(
         kernel,
-        out_shape=(
-            jax.ShapeDtypeStruct((RANK, D), F32),
-            jax.ShapeDtypeStruct((RANK, 6144), F32),
-        ),
+        out_shape=jax.ShapeDtypeStruct((4, 8, 8, 1920), BF16),
         in_specs=[vmem, vmem, vmem, vmem, vmem, pl.BlockSpec(memory_space=pl.ANY),
                   pl.BlockSpec(memory_space=pltpu.SMEM), vmem],
-        out_specs=(vmem, vmem),
+        out_specs=vmem,
         scratch_shapes=[
             pltpu.VMEM((2, 48, 128), BF16),
             pltpu.VMEM((2, 48, 256), BF16),
-            pltpu.VMEM((2, 8, 8, 48, 128), BF16),
+            pltpu.VMEM((2, 2, 4, 8, 48, 128), BF16),
             pltpu.VMEM((2, 2, 4, 8, 48, 256), BF16),
             pltpu.VMEM((4, 2, ROWS, WIDE), BF16),
             pltpu.VMEM((2, 2, RANK, 384), BF16),
@@ -530,17 +533,25 @@
             pltpu.VMEM((8, 2, 8, 768), BF16),
             pltpu.VMEM((8, 8, 384), BF16),
             pltpu.VMEM((8, 8, 384), BF16),
-            pltpu.VMEM((4, 8, 8, 1920), BF16),
-            dma((3,)), dma((3,)), dma((6,)), dma((6,)), dma((8,)), dma((8,)), dma((4,)), dma((2,)),
-            dma((6,)), dma((6,)), dma((2, 9)), dma((2, 9)), dma((2, 9)), dma((2, 9)),
-            dma((2, 16)), dma((2, 16)), dma((2, 16)), dma((2, 16)),
+            dma((4,)), dma((4,)), dma((1,)), dma((1,)), dma((6,)), dma((6,)), dma((8,)), dma((8,)), dma((4,)), dma((2,)),
+            dma((2, 2, 9)), dma((2, 2, 9)), dma((2, 2, 9)), dma((2, 2, 9)),
+            dma((3, 16)), dma((3, 16)), dma((2, 16)), dma((2, 16)),
             dma((4, 2)), dma((4, 2)), dma((4,)), dma((4,)), dma((8, 2)), dma((8, 2)),
             dma((8,)), dma((8,)), dma((8,)), dma((8,)), dma((6,)), dma((6,)),
         ],
         compiler_params=pltpu.CompilerParams(
             collective_id=0, has_side_effects=True, vmem_limit_bytes=56 * 1024 * 1024
         ),
-    )(frames, gain.reshape(1, D), w1, w2, down_map, up_map, lengths, cot)
+    )(frames, gain, w1, w2.T, down_map[0].T, up_map, lengths, cot)
+    dn, up = pl.pallas_call(
+        spread,
+        out_shape=(
+            jax.ShapeDtypeStruct((RANK, D), F32),
+            jax.ShapeDtypeStruct((RANK, 6144), F32),
+        ),
+        in_specs=[vmem],
+        out_specs=(vmem, vmem),
+    )(pieces)
     return dn.T[None], up[None]
 
 

time: 126 us -> 110 us (0.87)
  local copies, waits for them, and re-layouts: 9.08 us -> 0 us
  Pallas kernels: 115 us -> 109 us
    unnamed x4 -> x0, local copies, waits for them, and re-layouts: 7.79 us -> none
    pallas_call x1 -> x2, Pallas kernels: 115 us -> 109 us  [the longest x1 106 us: on_device(): pl.pallas_call(kernel, out_shape=jax.ShapeDtypeStruct((4, 8, 8, 1920), BF...]
    reshape x1 -> x0, local copies, waits for them, and re-layouts: 1.29 us -> none  [on_device(): gain.reshape(1, D)]
where the time goes in v2:
time: 110 us
  Pallas kernels  109 us (99%)
  between operations  1.29 us (1%)
    pallas_call x1, Pallas kernels, on_device(): pl.pallas_call(kernel, out_shape=jax.ShapeDtypeStruct((4, 8, 8, 1920), BF...  106 us
    pallas_call x1, Pallas kernels, on_device(): pl.pallas_call(spread, out_shape=(jax.ShapeDtypeStruct((RANK, D), F32), j...  2.62 us

profile of v2, /device:TPU:32, one launch (start us, length us, event | category | flops | bytes accessed | tf_op | source)
XLA Modules:
  0.0 110.1 jit_solution(4593853731973605075)
XLA Ops:
  1.3 106.2 %shard_map.95.ag = bf16[4,8,8,1920]{3,2,1,0:T(8,128)(2,1)} custom-call(bf16[1,144,1536]{2,1,0:T(8,128)(2,1)} %frames.1, f32[1536]{0:T(1024)} %gain.1, bf16[48,384]{1,0:T(8,128)(2,1)} %w1.1, bf16[48,384]{1,0:T(8,128)(2,1)} %bitcast.9, bf16[64,1536]{1,0:T(8,128)(2,1)} %bitcast.8, bf16[1,64,6144]{2,1,0:T(8,128)(2,1)} %up_map.1, s32[1,1]{1,0:T(1,128)S(6)} %copy.10.lengths, ...), custom_call_target="tpu_custom_call" | custom-call | tf_op jit(solution)/shard_map/pallas_call | solution.py:516
  107.5 2.6 %shard_map.96 = (f32[64,1536]{1,0:T(8,128)}, f32[64,6144]{1,0:T(8,128)}) custom-call(bf16[4,8,8,1920]{3,2,1,0:T(8,128)(2,1)} %shard_map.95.ag), custom_call_target="tpu_custom_call" | custom-call | tf_op jit(solution)/shard_map/pallas_call | solution.py:546

commit v3 on v2

v3 whole, which is shorter than its diff:
```python
import jax
import jax.numpy as jnp
from jax import lax
from jax.experimental import pallas as pl
from jax.experimental.pallas import tpu as pltpu
from jax.sharding import PartitionSpec as P

MESH = pl.DeviceIdType.MESH
ROWS = 128
D = 1536
RANK = 64
LOW = D
COT = D + 128
WIDE = 2 * D + 128
F32 = jnp.float32
BF16 = jnp.bfloat16


def dot(a, b, dims=((1,), (0,))):
    return lax.dot_general(a, b, (dims, ((), ())), preferred_element_type=F32)


def kernel(
    frames, gain, w1, w2t, down_map, up_map, lengths, cot,
    agu, agd,
    ws_a, ws_b, wa, wb, tok, ub, bks, bkr, bka, rss, rsr, dns, dnr,
    ta_s, ta_r, tb_s, tb_r, tk_s, tk_r, td_s, td_r, u_s, u_r,
    az_s, az_r, bz_s, bz_r, by_s, by_r, bo_s, bo_r,
    bk_s, bk_r, ba_s, ba_r, rs_s, rs_r, dn_s, dn_r, gz_s, gz_r, gx_s, gx_r,
):
    fi = lax.axis_index("fsdp")
    mi = lax.axis_index("member")
    x, zl = fi // 8, fi % 8
    y, zh, c = mi // 4, (mi // 2) % 2, mi % 2
    z = zh * 8 + zl

    def dev(x_, y_, z_, c_):
        return (x_ * 8 + z_ % 8, y_ * 4 + (z_ // 8) * 2 + c_)

    xr, xl, xo = (x + 1) % 4, (x + 3) % 4, (x + 2) % 4
    yr, yl, yo = (y + 1) % 4, (y + 3) % 4, (y + 2) % 4
    right, left = dev(xr, y, z, c), dev(xl, y, z, c)
    up, dn = dev(x, yr, z, c), dev(x, yl, z, c)
    fore, aft = dev(x, y, (z + 1) % 16, c), dev(x, y, (z + 15) % 16, c)
    twin = dev(x, y, z, 1 - c)
    flip = dev(y, x, z, c)

    def zdev(d, c_):
        return dev(x, y, zh * 8 + (zl + d) % 8, c_)

    def rcopy(src, dst, ss, rs, to):
        return pltpu.make_async_remote_copy(
            src_ref=src, dst_ref=dst, send_sem=ss, recv_sem=rs, device_id=to, device_id_type=MESH
        )

    def sent(ref, sem):
        rcopy(ref, ref, sem, sem, right).wait_send()

    def got(ref, sem):
        rcopy(ref, ref, sem, sem, right).wait_recv()

    barrier = pltpu.get_barrier_semaphore()
    peers = [up, dn, dev(x, yo, z, c), fore, aft, twin]
    for d in range(1, 4):
        for c_ in range(2):
            peers.append(dev((x + d) % 4, y, z, c_))
    for d in range(1, 8):
        for c_ in range(2):
            peers.append(zdev(d, c_))
    for peer in peers:
        pl.semaphore_signal(barrier, inc=1, device_id=peer, device_id_type=MESH)

    for e in range(1, 4):
        peer = dev((x + e) % 4, x, z, c)
        pl.semaphore_signal(barrier, inc=1, device_id=peer, device_id_type=MESH)

    @pl.when(x != y)
    def _():
        pl.semaphore_signal(barrier, inc=1, device_id=dev(x, x, z, c), device_id_type=MESH)
        pl.semaphore_signal(barrier, inc=1, device_id=flip, device_id_type=MESH)

    ws_a[0] = w1[:, 0:128]
    ws_b[0] = w1[:, 128:384]
    ws_a[1] = w2t[:, 0:128]
    ws_b[1] = w2t[:, 128:384]

    pl.semaphore_wait(barrier, len(peers) + jnp.where(x != y, 5, 3))

    def ta_copy(e):
        to = dev(y, (y + e) % 4, z, c)
        return rcopy(ws_a, wa.at[zh, :, x, zl], ta_s.at[e], ta_r.at[x], to)

    def ta_wait(a):
        slot = wa.at[zh, :, a, zl]
        rcopy(slot, slot, ta_s.at[0], ta_r.at[a], flip).wait_recv()

    def tb_copy():
        return rcopy(ws_b, wb.at[zh, :, x, zl], tb_s.at[0], tb_r.at[0], flip)

    @pl.when(x != y)
    def _():
        tb_copy().start()
        ta_copy(0).start()

    @pl.when(x == y)
    def _():
        for w in range(2):
            wa[zh, w, y, zl] = ws_a[w]
            wb[zh, w, y, zl] = ws_b[w]

    for e in range(1, 4):
        ta_copy(e).start()

    v = frames[0, 0:ROWS, :].astype(F32)
    mean = jnp.mean(v, axis=1, keepdims=True)
    var = jnp.mean((v - mean) ** 2, axis=1, keepdims=True)
    normed = (gain[...][None, :] * (v - mean) / jnp.sqrt(var + 1e-05)).astype(BF16)
    low = dot(normed, down_map[...], ((1,), (1,))).astype(BF16)
    keep = lax.broadcasted_iota(jnp.int32, (ROWS, D), 0) < lengths[0, 0]
    masked = jnp.where(keep, cot[0, 0:ROWS, :].astype(F32), 0.0).astype(BF16)
    tok[x, c, :, 0:D] = normed
    tok[x, c, :, LOW : LOW + 128] = jnp.concatenate([low, jnp.zeros_like(low)], axis=1)
    tok[x, c, :, COT:WIDE] = masked

    def half(x_, h):
        return tok.at[x_, c, pl.ds(64 * h, 64), :]

    def halfo(x_, h):
        return tok.at[x_, 1 - c, pl.ds(64 * h, 64), :]

    def t_copy(i):
        x_, h, to = [
            (x, 0, right), (x, 1, right), (x, 1, left), (x, 0, left), (xl, 0, right), (xr, 1, left)
        ][i]
        return rcopy(half(x_, h), half(x_, h), tk_s.at[0], tk_r.at[i], to)

    def t_wait(i):
        x_, h = [(xl, 0), (xl, 1), (xr, 1), (xr, 0), (xo, 0), (xo, 1)][i]
        got(half(x_, h), tk_r.at[i])

    def d_copy(r, h):
        x_ = [x, xl, xr, xo][r]
        return rcopy(half(x_, h), half(x_, h), td_s.at[0], td_r.at[0], twin)

    for i in (0, 2, 1, 3):
        t_copy(i).start()

    def a_str(s, w):
        z_ = (z + s + 16) % 16
        return wa.at[z_ // 8, w, :, z_ % 8]

    def b_str(s, w):
        return b_half(s, y, w)

    def b_blk(s, y_):
        z_ = (z + s + 16) % 16
        return wb.at[z_ // 8, :, y_, z_ % 8]

    def b_half(s, y_, w):
        z_ = (z + s + 16) % 16
        return wb.at[z_ // 8, w, y_, z_ % 8]

    streams = [(b_str, bz_s, bz_r), (a_str, az_s, az_r)]

    def z_copy(i, w, route, k):
        make, ss, rs = streams[i]
        blk = make((-(k - 1)) if route == 0 else (k - 1), w)
        return rcopy(blk, blk, ss.at[route], rs.at[route, w, k - 1], fore if route == 0 else aft)

    def z_wait(i, w, route, k):
        make, ss, rs = streams[i]
        blk = make(-k if route == 0 else k, w)
        got(blk, rs.at[route, w, k - 1])

    def by_copy(s, j, way):
        return rcopy(b_blk(s, y), b_blk(s, y), by_s.at[way], by_r.at[way, j], up if way == 0 else dn)

    def by_wait(s, j, way):
        y_ = yl if way == 0 else yr
        got(b_blk(s, y_), by_r.at[way, j])

    def by_last(way):
        blk = b_blk(8, y)
        return rcopy(blk, blk, by_s.at[way], by_r.at[way, 15], [up, dn, dev(x, yo, z, c)][way])

    def by_last_wait(way):
        blk = b_blk(8, [yl, yr, yo][way])
        got(blk, by_r.at[way, 15])

    def bo_copy(s, way):
        y_ = yl if way == 0 else yr
        return rcopy(
            b_half(s, y_, way), b_half(s, y_, way), bo_s.at[way], bo_r.at[way], up if way == 0 else dn
        )

    @pl.when(x != y)
    def _():
        blk = wb.at[zh, :, y, zl]
        rcopy(blk, blk, tb_s.at[0], tb_r.at[0], flip).wait_recv()

    for w in range(2):
        for route in range(2):
            z_copy(0, w, route, 1).start()
    for way in range(2):
        by_copy(0, 0, way).start()
    for e in range(1, 4):
        ta_wait((x + e) % 4)

    @pl.when(x != y)
    def _():
        ta_wait(x)

    for w in range(2):
        for route in range(2):
            z_copy(1, w, route, 1).start()

    for h in range(2):
        d_copy(0, h).start()

    def u_cols(zh_, c_):
        return up_map.at[0, :, pl.ds(pl.multiple_of(((x * 2 + zh_) * 2 + c_) * 384, 128), 384)]

    def u_local(zh_):
        return pltpu.make_async_copy(u_cols(zh_, c), ub.at[c, zh_], u_s.at[2 + zh_])

    def u_copy(zh_):
        return rcopy(u_cols(zh_, 1 - c), ub.at[c, zh_], u_s.at[zh_], u_r.at[zh_], twin)

    for zh_ in range(2):
        u_local(zh_).start()
        u_copy(zh_).start()

    def y_stage(s, j):
        for way in range(2):
            by_wait(s, j, way)
            bo_copy(s, way).start()

    def step(k, _):
        for w in range(2):
            for route in range(2):
                z_wait(0, w, route, k)
                z_copy(0, w, route, k + 1).start()
        for route in range(2):
            for way in range(2):
                by_copy(-k if route == 0 else k, 2 * k - 1 + route, way).start()
        for w in range(2):
            for route in range(2):
                z_wait(1, w, route, k)
                z_copy(1, w, route, k + 1).start()
        for route in range(2):
            s = -(k - 1) if route == 0 else (k - 1)

            @pl.when((k > 1) | (route == 0))
            def _():
                y_stage(s, jnp.where(k == 1, 0, 2 * k - 3 + route))
        return 0

    lax.fori_loop(1, 4, step, 0)
    t_wait(0)
    t_copy(4).start()
    d_copy(1, 0).start()
    t_wait(2)
    t_copy(5).start()
    d_copy(2, 1).start()
    lax.fori_loop(4, 7, step, 0)
    t_wait(1)
    d_copy(1, 1).start()
    t_wait(3)
    d_copy(2, 0).start()
    for w in range(2):
        for route in range(2):
            z_wait(0, w, route, 7)
            if route == w:
                z_copy(0, w, route, 8).start()
    for route in range(2):
        for way in range(2):
            by_copy(-7 if route == 0 else 7, 13 + route, way).start()
    for w in range(2):
        for route in range(2):
            z_wait(1, w, route, 7)
            if route == w:
                z_copy(1, w, route, 8).start()
    y_stage(-6, 11)
    y_stage(6, 12)
    for w in range(2):
        z_wait(0, w, w, 8)
    for way in range(3):
        by_last(way).start()
    y_stage(-7, 13)
    y_stage(7, 14)
    for i in (4, 5):
        t_wait(i)
        d_copy(3, i - 4).start()
    for w in range(2):
        z_wait(1, w, w, 8)
    for way in range(3):
        by_last_wait(way)

    for way in range(2):
        got(wb.at[0, 0, 0:3, 0:5], bo_r.at[way])
    got(tok.at[:, 0], td_r.at[0])
    for zh_ in range(2):
        u_local(zh_).wait()
        rcopy(ub.at[1 - c, zh_], ub.at[1 - c, zh_], u_s.at[zh_], u_r.at[zh_], twin).wait_recv()

    def half_of(zh_):
        def member(m, _):
            lo = tok[:, m, :, LOW : LOW + 128].reshape(4 * ROWS, 128)
            for is_b in range(2):
                c0, c1 = (128, 384) if is_b else (0, 128)
                if is_b:
                    wi, wo = wb[zh_, 0].reshape(D, 256), wb[zh_, 1].reshape(D, 256)
                else:
                    wi, wo = wa[zh_, 0].reshape(D, 128), wa[zh_, 1].reshape(D, 128)
                u = ub[m, zh_, :, c0:c1]
                pre = dot(tok[:, m, :, 0:D].reshape(4 * ROWS, D), wi) + dot(lo[:, 0:RANK], u)
                dhid = 0.5 * dot(tok[:, m, :, COT:WIDE].reshape(4 * ROWS, D), wo)
                sig = jax.nn.sigmoid(pre)
                dpre = (dhid * sig * (1.0 + pre * (1.0 - sig))).astype(BF16)
                part = dot(lo, dpre, ((0,), (0,)))
                for r in range(8):
                    rss[zh_, m, r, :, c0:c1] = part[8 * r : 8 * r + 8].astype(BF16)
                for x_ in range(4):
                    bp = dot(u, dpre[ROWS * x_ : ROWS * (x_ + 1)], ((1,), (1,)))
                    if zh_ == 0 and is_b == 0:
                        bks[x_, m] = bp
                    else:
                        bks[x_, m] += bp
            return 0

        lax.fori_loop(0, 2, member, 0)

    def rs_copy(g, d, c_):
        return rcopy(
            rss.at[g, c_, (zl + d) % 8], rsr.at[g, zl, c], rs_s.at[g, c_], rs_r.at[g, c], zdev(d, c_)
        )

    def rs_other(g):
        return rcopy(rss.at[g, 1 - c, zl], rsr.at[g, zl, c], rs_s.at[g, 2], rs_r.at[g, 2], twin)

    def rs_start(g):
        for d in (4, 3, 5, 2, 6, 1, 7):
            for c_ in range(2):
                rs_copy(g, d, c_).start()
        rs_other(g).start()
        rsr[g, zl, c] = rss[g, c, zl]

    def rs_sum(g):
        got(rsr.at[g, zl, 1 - c], rs_r.at[g, 2])
        for c_ in range(2):
            got(rsr.at[g, 0:7, c_], rs_r.at[g, c_])
        for c_ in range(2):
            total = rsr[g, 0, c_].astype(F32)
            for i in range(1, 8):
                total = total + rsr[g, i, c_].astype(F32)
            agu[g, x, zl, :, 384 * c_ : 384 * (c_ + 1)] = total.astype(BF16)

    def bk_copy(d, c_):
        x_ = (x + d) % 4
        return rcopy(bks.at[x_, c_], bkr.at[x, c], bk_s.at[c_], bk_r.at[c], dev(x_, y, z, c_))

    def bk_other():
        return rcopy(bks.at[x, 1 - c], bkr.at[x, c], bk_s.at[2], bk_r.at[2], twin)

    def ba_copy(d):
        return rcopy(bka.at[x], bka.at[x], ba_s.at[0], ba_r.at[0], dev((x + d) % 4, y, z, c))

    def dn_copy(d):
        return rcopy(dns.at[(zl + d) % 8], dnr.at[zl], dn_s.at[0], dn_r.at[0], zdev(d, c))

    z4, q4 = (zl // 4) * 4, zl % 4
    far = (zl + 4) % 8

    def piece(g, zl_):
        return agd.at[x, zl_] if g == 2 else agu.at[g, x, zl_]

    def near(j):
        return dev(x, y, zh * 8 + z4 + (q4 + j) % 4, c)

    def gz_copy(g, j):
        if j == 0:
            return rcopy(piece(g, zl), piece(g, zl), gz_s.at[g], gz_r.at[g, 0], dev(x, y, zh * 8 + far, c))
        src = zl if j < 4 else far
        return rcopy(piece(g, src), piece(g, src), gz_s.at[g], gz_r.at[g, 1 if j < 4 else 2], near((j - 1) % 3 + 1))

    def gz_wait(g, i):
        slots = agd.at[0] if g == 2 else agu.at[g, 0]
        got(slots.at[0:1] if i == 0 else slots.at[0:3], gz_r.at[g, i])

    def g_half(g, x_, h):
        return agu.at[g, x_, pl.ds(z4 if h == 0 else 4 - z4, 4)]

    def gx_copy(g, i):
        x_, h, to = [
            (x, 0, right), (x, 1, right), (x, 1, left), (x, 0, left), (xl, 0, right), (xr, 1, left)
        ][i]
        return rcopy(g_half(g, x_, h), g_half(g, x_, h), gx_s.at[g], gx_r.at[g, i], to)

    def gx_wait(g, i):
        x_, h = [(xl, 0), (xl, 1), (xr, 1), (xr, 0), (xo, 0), (xo, 1)][i]
        got(g_half(g, x_, h), gx_r.at[g, i])

    def gd_copy(d):
        return rcopy(agd.at[x], agd.at[x], gx_s.at[2], gx_r.at[2, 0], dev((x + d) % 4, y, z, c))

    def gz_own(g):
        for j in range(4):
            gz_copy(g, j).start()

    def gz_pass(g):
        gz_wait(g, 0)
        for j in range(4, 7):
            gz_copy(g, j).start()

    def gx_first(g):
        gz_wait(g, 1)
        gx_copy(g, 0).start()
        gx_copy(g, 3).start()

    def gx_second(g):
        gz_wait(g, 2)
        gx_copy(g, 2).start()
        gx_copy(g, 1).start()

    def gx_pass(g):
        gx_wait(g, 0)
        gx_copy(g, 4).start()
        gx_wait(g, 2)
        gx_copy(g, 5).start()

    half_of(0)
    rs_start(0)
    half_of(1)
    for d in range(1, 4):
        for c_ in range(2):
            bk_copy(d, c_).start()
    bk_other().start()
    rs_start(1)
    bkr[x, c] = bks[x, c]

    got(bkr.at[x, 1 - c], bk_r.at[2])
    for c_ in range(2):
        got(bkr.at[0:3, c_], bk_r.at[c_])
    total = bkr[0, 0]
    for i in range(1, 8):
        total = total + bkr[i // 2, i % 2]
    bka[x] = total.astype(BF16)
    for d in range(1, 4):
        ba_copy(d).start()

    rs_sum(0)
    gz_own(0)

    got(bka.at[0:3], ba_r.at[0])
    quarter = pl.ds(pl.multiple_of(x * 384, 128), 384)
    part = dot(bka[0], tok[0, c, :, quarter])
    for x_ in range(1, 4):
        part = part + dot(bka[x_], tok[x_, c, :, quarter])
    for r in range(8):
        dns[r] = part[8 * r : 8 * r + 8].astype(BF16)
    for d in range(1, 8):
        dn_copy(d).start()
    dnr[zl] = dns[zl]

    rs_sum(1)
    gz_own(1)
    gz_pass(0)
    gx_first(0)
    got(dnr.at[0:7], dn_r.at[0])
    total = dnr[0].astype(F32)
    for i in range(1, 8):
        total = total + dnr[i].astype(F32)
    agd[x, zl] = total.astype(BF16)
    gz_own(2)
    gz_pass(1)
    gx_second(0)
    gx_first(1)
    gz_pass(2)
    gx_pass(0)
    gx_second(1)
    gz_wait(2, 1)
    gz_wait(2, 2)
    for d in range(1, 4):
        gd_copy(d).start()
    gx_pass(1)
    for g in range(2):
        for i in (1, 3, 4, 5):
            gx_wait(g, i)
    got(agd.at[0:3], gx_r.at[2, 0])

    @pl.when(x != y)
    def _():
        tb_copy().wait_send()
        ta_copy(0).wait_send()

    for e in range(1, 4):
        ta_copy(e).wait_send()
    sent(tok.at[0:3, 0], tk_s.at[0])
    sent(tok.at[:, 0], td_s.at[0])
    for zh_ in range(2):
        u_copy(zh_).wait_send()
    for route in range(2):
        sent(wa.at[0:2, 0:2, 0:3, 0:5], az_s.at[route])
        sent(wb.at[0, 0, 0:3, 0:5], bz_s.at[route])
        sent(wb.at[0, 0], by_s.at[route])
        sent(wb.at[0, 0, 0:3, 0:5], bo_s.at[route])
    sent(wb.at[0, 0, 0, 0:2], by_s.at[2])
    bk_other().wait_send()
    for c_ in range(2):
        sent(bks.at[0:3, 0], bk_s.at[c_])
    sent(bka.at[0:3], ba_s.at[0])
    sent(dns.at[0:7], dn_s.at[0])
    for g in range(2):
        rs_other(g).wait_send()
        for c_ in range(2):
            sent(rss.at[g, c_, 0:7], rs_s.at[g, c_])
        sent(agu.at[g, 0, 0:7], gz_s.at[g])
        sent(agu.at[g, 0:3], gx_s.at[g])
    sent(agd.at[0, 0:7], gz_s.at[2])
    sent(agd.at[0:3], gx_s.at[2])


def spread(agu, agd, dn_out, up_out):
    def write(i, _):
        rows = pl.ds(pl.multiple_of(8 * i, 8), 8)
        for x_ in range(4):
            for c_ in range(2):
                for h in range(2):
                    col = ((x_ * 2 + h) * 2 + c_) * 384
                    up_out[rows, col : col + 384] = agu[h, x_, i, :, 384 * c_ : 384 * (c_ + 1)].astype(F32)
            dn_out[rows, 384 * x_ : 384 * (x_ + 1)] = agd[x_, i].astype(F32)
        return 0

    lax.fori_loop(0, 8, write, 0)


def on_device(frames, gain, w1, w2, down_map, up_map, lengths, cot):
    vmem = pl.BlockSpec(memory_space=pltpu.VMEM)
    dma = pltpu.SemaphoreType.DMA
    pieces = pl.pallas_call(
        kernel,
        out_shape=(
            jax.ShapeDtypeStruct((2, 4, 8, 8, 768), BF16),
            jax.ShapeDtypeStruct((4, 8, 8, 384), BF16),
        ),
        in_specs=[vmem, vmem, vmem, vmem, vmem, pl.BlockSpec(memory_space=pl.ANY),
                  pl.BlockSpec(memory_space=pltpu.SMEM), vmem],
        out_specs=(vmem, vmem),
        scratch_shapes=[
            pltpu.VMEM((2, 48, 128), BF16),
            pltpu.VMEM((2, 48, 256), BF16),
            pltpu.VMEM((2, 2, 4, 8, 48, 128), BF16),
            pltpu.VMEM((2, 2, 4, 8, 48, 256), BF16),
            pltpu.VMEM((4, 2, ROWS, WIDE), BF16),
            pltpu.VMEM((2, 2, RANK, 384), BF16),
            pltpu.VMEM((4, 2, RANK, ROWS), F32),
            pltpu.VMEM((4, 2, RANK, ROWS), F32),
            pltpu.VMEM((4, RANK, ROWS), BF16),
            pltpu.VMEM((2, 2, 8, 8, 384), BF16),
            pltpu.VMEM((2, 8, 2, 8, 384), BF16),
            pltpu.VMEM((8, 8, 384), BF16),
            pltpu.VMEM((8, 8, 384), BF16),
            dma((4,)), dma((4,)), dma((1,)), dma((1,)), dma((1,)), dma((6,)), dma((1,)), dma((1,)), dma((4,)), dma((2,)),
            dma((2,)), dma((2, 2, 8)), dma((2,)), dma((2, 2, 8)),
            dma((3,)), dma((3, 16)), dma((2,)), dma((2,)),
            dma((3,)), dma((3,)), dma((1,)), dma((1,)), dma((2, 3)), dma((2, 3)),
            dma((1,)), dma((1,)), dma((3,)), dma((3, 3)), dma((3,)), dma((3, 6)),
        ],
        compiler_params=pltpu.CompilerParams(
            collective_id=0, has_side_effects=True, vmem_limit_bytes=56 * 1024 * 1024
        ),
    )(frames, gain, w1, w2.T, down_map[0].T, up_map, lengths, cot)
    dn, up = pl.pallas_call(
        spread,
        out_shape=(
            jax.ShapeDtypeStruct((RANK, D), F32),
            jax.ShapeDtypeStruct((RANK, 6144), F32),
        ),
        in_specs=[vmem, vmem],
        out_specs=(vmem, vmem),
    )(*pieces)
    return dn.T[None], up[None]


def solution(mesh):
    in_specs = (
        P("member", "fsdp", None),
        P(),
        P("fsdp", "member"),
        P("member", "fsdp"),
        P("member", None, None),
        P("member", None, None),
        P("member", "fsdp"),
        P("member", "fsdp", None),
    )
    out_specs = (P("member", None, None), P("member", None, None))
    return jax.shard_map(
        on_device, mesh=mesh, in_specs=in_specs, out_specs=out_specs, check_vma=False
    )
```

time: 110 us -> 104 us (0.945)
  the two profiles are of different devices: /device:TPU:32 before, /device:TPU:8 now
where the time goes in v3:
time: 104 us; the launch traced here: 103 us
  Pallas kernels  102 us (98%)
  between operations  1.29 us (1%)
    pallas_call x1, Pallas kernels, on_device(): pl.pallas_call(kernel, out_shape=(jax.ShapeDtypeStruct((2, 4, 8, 8, 768),...  99.5 us
    pallas_call x1, Pallas kernels, on_device(): pl.pallas_call(spread, out_shape=(jax.ShapeDtypeStruct((RANK, D), F32), j...  2.59 us

profile of v3, /device:TPU:8, one launch (start us, length us, event | category | flops | bytes accessed | tf_op | source)
XLA Modules:
  0.0 103.4 jit_solution(9297907214793253575)
XLA Ops:
  1.3 99.5 %shard_map.95 = (bf16[2,4,8,8,768]{4,3,2,1,0:T(8,128)(2,1)}, bf16[4,8,8,384]{3,2,1,0:T(8,128)(2,1)}) custom-call(bf16[1,144,1536]{2,1,0:T(8,128)(2,1)} %frames.1, f32[1536]{0:T(1024)} %gain.1, bf16[48,384]{1,0:T(8,128)(2,1)} %w1.1, bf16[48,384]{1,0:T(8,128)(2,1)} %bitcast.9, bf16[64,1536]{1,0:T(8,128)(2,1)} %bitcast.8, bf16[1,64,6144]{2,1,0:T(8,128)(2,1)} %up_map.1, ...), custom_call_target="tpu_custom_call" | custom-call | tf_op jit(solution)/shard_map/pallas_call | solution.py:540
  100.8 2.6 %shard_map.96 = (f32[64,1536]{1,0:T(8,128)}, f32[64,6144]{1,0:T(8,128)}) custom-call(bf16[2,4,8,8,768]{4,3,2,1,0:T(8,128)(2,1)} %get-tuple-element.6.agu, bf16[4,8,8,384]{3,2,1,0:T(8,128)(2,1)} %get-tuple-element.7.agd), custom_call_target="tpu_custom_call" | custom-call | tf_op jit(solution)/shard_map/pallas_call | solution.py:573

commit v4 on v3

--- a/solution.py
+++ b/solution.py
@@ -86,12 +86,15 @@
 
     pl.semaphore_wait(barrier, len(peers) + jnp.where(x != y, 5, 3))
 
+    def lanes(zh_):
+        return pl.ds(pl.multiple_of(zh_ * 128, 128), 128)
+
     def ta_copy(e):
         to = dev(y, (y + e) % 4, z, c)
-        return rcopy(ws_a, wa.at[zh, :, x, zl], ta_s.at[e], ta_r.at[x], to)
+        return rcopy(ws_a, wa.at[:, x, zl, :, lanes(zh)], ta_s.at[e], ta_r.at[x], to)
 
     def ta_wait(a):
-        slot = wa.at[zh, :, a, zl]
+        slot = wa.at[:, a, zl, :, lanes(zh)]
         rcopy(slot, slot, ta_s.at[0], ta_r.at[a], flip).wait_recv()
 
     def tb_copy():
@@ -105,7 +108,7 @@
     @pl.when(x == y)
     def _():
         for w in range(2):
-            wa[zh, w, y, zl] = ws_a[w]
+            wa[w, y, zl, :, lanes(zh)] = ws_a[w]
             wb[zh, w, y, zl] = ws_b[w]
 
     for e in range(1, 4):
@@ -147,7 +150,7 @@
 
     def a_str(s, w):
         z_ = (z + s + 16) % 16
-        return wa.at[z_ // 8, w, :, z_ % 8]
+        return wa.at[w, :, z_ % 8, :, lanes(z_ // 8)]
 
     def b_str(s, w):
         return b_half(s, y, w)
@@ -303,29 +306,28 @@
         u_local(zh_).wait()
         rcopy(ub.at[1 - c, zh_], ub.at[1 - c, zh_], u_s.at[zh_], u_r.at[zh_], twin).wait_recv()
 
-    def half_of(zh_):
+    def third(g):
         def member(m, _):
             lo = tok[:, m, :, LOW : LOW + 128].reshape(4 * ROWS, 128)
-            for is_b in range(2):
-                c0, c1 = (128, 384) if is_b else (0, 128)
-                if is_b:
-                    wi, wo = wb[zh_, 0].reshape(D, 256), wb[zh_, 1].reshape(D, 256)
+            if g < 2:
+                wi, wo = wb[g, 0].reshape(D, 256), wb[g, 1].reshape(D, 256)
+                u = ub[m, g, :, 128:384]
+            else:
+                wi, wo = wa[0].reshape(D, 256), wa[1].reshape(D, 256)
+                u = jnp.concatenate([ub[m, 0, :, 0:128], ub[m, 1, :, 0:128]], axis=1)
+            pre = dot(tok[:, m, :, 0:D].reshape(4 * ROWS, D), wi) + dot(lo[:, 0:RANK], u)
+            dhid = 0.5 * dot(tok[:, m, :, COT:WIDE].reshape(4 * ROWS, D), wo)
+            sig = jax.nn.sigmoid(pre)
+            dpre = (dhid * sig * (1.0 + pre * (1.0 - sig))).astype(BF16)
+            part = dot(lo, dpre, ((0,), (0,)))
+            for r in range(8):
+                rss[g, m, r] = part[8 * r : 8 * r + 8].astype(BF16)
+            for x_ in range(4):
+                bp = dot(u, dpre[ROWS * x_ : ROWS * (x_ + 1)], ((1,), (1,)))
+                if g == 0:
+                    bks[x_, m] = bp
                 else:
-                    wi, wo = wa[zh_, 0].reshape(D, 128), wa[zh_, 1].reshape(D, 128)
-                u = ub[m, zh_, :, c0:c1]
-                pre = dot(tok[:, m, :, 0:D].reshape(4 * ROWS, D), wi) + dot(lo[:, 0:RANK], u)
-                dhid = 0.5 * dot(tok[:, m, :, COT:WIDE].reshape(4 * ROWS, D), wo)
-                sig = jax.nn.sigmoid(pre)
-                dpre = (dhid * sig * (1.0 + pre * (1.0 - sig))).astype(BF16)
-                part = dot(lo, dpre, ((0,), (0,)))
-                for r in range(8):
-                    rss[zh_, m, r, :, c0:c1] = part[8 * r : 8 * r + 8].astype(BF16)
-                for x_ in range(4):
-                    bp = dot(u, dpre[ROWS * x_ : ROWS * (x_ + 1)], ((1,), (1,)))
-                    if zh_ == 0 and is_b == 0:
-                        bks[x_, m] = bp
-                    else:
-                        bks[x_, m] += bp
+                    bks[x_, m] += bp
             return 0
 
         lax.fori_loop(0, 2, member, 0)
@@ -353,7 +355,7 @@
             total = rsr[g, 0, c_].astype(F32)
             for i in range(1, 8):
                 total = total + rsr[g, i, c_].astype(F32)
-            agu[g, x, zl, :, 384 * c_ : 384 * (c_ + 1)] = total.astype(BF16)
+            agu[g, x, zl, :, 256 * c_ : 256 * (c_ + 1)] = total.astype(BF16)
 
     def bk_copy(d, c_):
         x_ = (x + d) % 4
@@ -372,7 +374,7 @@
     far = (zl + 4) % 8
 
     def piece(g, zl_):
-        return agd.at[x, zl_] if g == 2 else agu.at[g, x, zl_]
+        return agd.at[x, zl_] if g == 3 else agu.at[g, x, zl_]
 
     def near(j):
         return dev(x, y, zh * 8 + z4 + (q4 + j) % 4, c)
@@ -384,8 +386,14 @@
         return rcopy(piece(g, src), piece(g, src), gz_s.at[g], gz_r.at[g, 1 if j < 4 else 2], near((j - 1) % 3 + 1))
 
     def gz_wait(g, i):
-        slots = agd.at[0] if g == 2 else agu.at[g, 0]
-        got(slots.at[0:1] if i == 0 else slots.at[0:3], gz_r.at[g, i])
+        got(agu.at[g, 0, 0:1] if i == 0 else agu.at[g, 0, 0:3], gz_r.at[g, i])
+
+    def gz_all(g):
+        for d in (4, 3, 5, 2, 6, 1, 7):
+            rcopy(piece(g, zl), piece(g, zl), gz_s.at[g], gz_r.at[g, 0], zdev(d, c)).start()
+
+    def gz_all_wait(g):
+        got(agd.at[0, 0:7] if g == 3 else agu.at[g, 0, 0:7], gz_r.at[g, 0])
 
     def g_half(g, x_, h):
         return agu.at[g, x_, pl.ds(z4 if h == 0 else 4 - z4, 4)]
@@ -401,7 +409,7 @@
         got(g_half(g, x_, h), gx_r.at[g, i])
 
     def gd_copy(d):
-        return rcopy(agd.at[x], agd.at[x], gx_s.at[2], gx_r.at[2, 0], dev((x + d) % 4, y, z, c))
+        return rcopy(agd.at[x], agd.at[x], gx_s.at[3], gx_r.at[3, 0], dev((x + d) % 4, y, z, c))
 
     def gz_own(g):
         for j in range(4):
@@ -428,14 +436,16 @@
         gx_wait(g, 2)
         gx_copy(g, 5).start()
 
-    half_of(0)
+    third(0)
     rs_start(0)
-    half_of(1)
+    third(1)
+    rs_start(1)
+    third(2)
     for d in range(1, 4):
         for c_ in range(2):
             bk_copy(d, c_).start()
     bk_other().start()
-    rs_start(1)
+    rs_start(2)
     bkr[x, c] = bks[x, c]
 
     got(bkr.at[x, 1 - c], bk_r.at[2])
@@ -450,6 +460,8 @@
 
     rs_sum(0)
     gz_own(0)
+    rs_sum(1)
+    gz_own(1)
 
     got(bka.at[0:3], ba_r.at[0])
     quarter = pl.ds(pl.multiple_of(x * 384, 128), 384)
@@ -462,31 +474,33 @@
         dn_copy(d).start()
     dnr[zl] = dns[zl]
 
-    rs_sum(1)
-    gz_own(1)
+    rs_sum(2)
+    gz_all(2)
     gz_pass(0)
     gx_first(0)
+    gz_pass(1)
+    gx_first(1)
+    gx_second(0)
     got(dnr.at[0:7], dn_r.at[0])
     total = dnr[0].astype(F32)
     for i in range(1, 8):
         total = total + dnr[i].astype(F32)
     agd[x, zl] = total.astype(BF16)
-    gz_own(2)
-    gz_pass(1)
-    gx_second(0)
-    gx_first(1)
-    gz_pass(2)
+    gz_all(3)
+    gx_second(1)
     gx_pass(0)
-    gx_second(1)
-    gz_wait(2, 1)
-    gz_wait(2, 2)
+    gz_all_wait(2)
+    for i in (0, 2, 3, 1):
+        gx_copy(2, i).start()
+    gx_pass(1)
+    gz_all_wait(3)
     for d in range(1, 4):
         gd_copy(d).start()
-    gx_pass(1)
-    for g in range(2):
+    gx_pass(2)
+    for g in range(3):
         for i in (1, 3, 4, 5):
             gx_wait(g, i)
-    got(agd.at[0:3], gx_r.at[2, 0])
+    got(agd.at[0:3], gx_r.at[3, 0])
 
     @pl.when(x != y)
     def _():
@@ -500,7 +514,7 @@
     for zh_ in range(2):
         u_copy(zh_).wait_send()
     for route in range(2):
-        sent(wa.at[0:2, 0:2, 0:3, 0:5], az_s.at[route])
+        sent(wa.at[0:2, 0:3, 0:5], az_s.at[route])
         sent(wb.at[0, 0, 0:3, 0:5], bz_s.at[route])
         sent(wb.at[0, 0], by_s.at[route])
         sent(wb.at[0, 0, 0:3, 0:5], bo_s.at[route])
@@ -510,14 +524,14 @@
         sent(bks.at[0:3, 0], bk_s.at[c_])
     sent(bka.at[0:3], ba_s.at[0])
     sent(dns.at[0:7], dn_s.at[0])
-    for g in range(2):
+    for g in range(3):
         rs_other(g).wait_send()
         for c_ in range(2):
             sent(rss.at[g, c_, 0:7], rs_s.at[g, c_])
         sent(agu.at[g, 0, 0:7], gz_s.at[g])
         sent(agu.at[g, 0:3], gx_s.at[g])
-    sent(agd.at[0, 0:7], gz_s.at[2])
-    sent(agd.at[0:3], gx_s.at[2])
+    sent(agd.at[0, 0:7], gz_s.at[3])
+    sent(agd.at[0:3], gx_s.at[3])
 
 
 def spread(agu, agd, dn_out, up_out):
@@ -525,9 +539,11 @@
         rows = pl.ds(pl.multiple_of(8 * i, 8), 8)
         for x_ in range(4):
             for c_ in range(2):
+                lo = 256 * c_
                 for h in range(2):
                     col = ((x_ * 2 + h) * 2 + c_) * 384
-                    up_out[rows, col : col + 384] = agu[h, x_, i, :, 384 * c_ : 384 * (c_ + 1)].astype(F32)
+                    up_out[rows, col : col + 128] = agu[2, x_, i, :, lo + 128 * h : lo + 128 * (h + 1)].astype(F32)
+                    up_out[rows, col + 128 : col + 384] = agu[h, x_, i, :, lo : lo + 256].astype(F32)
             dn_out[rows, 384 * x_ : 384 * (x_ + 1)] = agd[x_, i].astype(F32)
         return 0
 
@@ -540,7 +556,7 @@
     pieces = pl.pallas_call(
         kernel,
         out_shape=(
-            jax.ShapeDtypeStruct((2, 4, 8, 8, 768), BF16),
+            jax.ShapeDtypeStruct((3, 4, 8, 8, 512), BF16),
             jax.ShapeDtypeStruct((4, 8, 8, 384), BF16),
         ),
         in_specs=[vmem, vmem, vmem, vmem, vmem, pl.BlockSpec(memory_space=pl.ANY),
@@ -549,22 +565,22 @@
         scratch_shapes=[
             pltpu.VMEM((2, 48, 128), BF16),
             pltpu.VMEM((2, 48, 256), BF16),
-            pltpu.VMEM((2, 2, 4, 8, 48, 128), BF16),
+            pltpu.VMEM((2, 4, 8, 48, 256), BF16),
             pltpu.VMEM((2, 2, 4, 8, 48, 256), BF16),
             pltpu.VMEM((4, 2, ROWS, WIDE), BF16),
             pltpu.VMEM((2, 2, RANK, 384), BF16),
             pltpu.VMEM((4, 2, RANK, ROWS), F32),
             pltpu.VMEM((4, 2, RANK, ROWS), F32),
             pltpu.VMEM((4, RANK, ROWS), BF16),
-            pltpu.VMEM((2, 2, 8, 8, 384), BF16),
-            pltpu.VMEM((2, 8, 2, 8, 384), BF16),
+            pltpu.VMEM((3, 2, 8, 8, 256), BF16),
+            pltpu.VMEM((3, 8, 2, 8, 256), BF16),
             pltpu.VMEM((8, 8, 384), BF16),
             pltpu.VMEM((8, 8, 384), BF16),
             dma((4,)), dma((4,)), dma((1,)), dma((1,)), dma((1,)), dma((6,)), dma((1,)), dma((1,)), dma((4,)), dma((2,)),
             dma((2,)), dma((2, 2, 8)), dma((2,)), dma((2, 2, 8)),
             dma((3,)), dma((3, 16)), dma((2,)), dma((2,)),
-            dma((3,)), dma((3,)), dma((1,)), dma((1,)), dma((2, 3)), dma((2, 3)),
-            dma((1,)), dma((1,)), dma((3,)), dma((3, 3)), dma((3,)), dma((3, 6)),
+            dma((3,)), dma((3,)), dma((1,)), dma((1,)), dma((3, 3)), dma((3, 3)),
+            dma((1,)), dma((1,)), dma((4,)), dma((4, 3)), dma((4,)), dma((4, 6)),
         ],
         compiler_params=pltpu.CompilerParams(
             collective_id=0, has_side_effects=True, vmem_limit_bytes=56 * 1024 * 1024

time: 104 us -> 100 us (0.962)
  Pallas kernels: 102 us -> 98.7 us
    pallas_call x1, Pallas kernels: 99.5 us -> 96.1 us  [on_device(): pl.pallas_call(kernel, out_shape=(jax.ShapeDtypeStruct((3, 4, 8, 8, 512),...]
where the time goes in v4:
time: 100 us; the launch traced here: 99.9 us
  Pallas kernels  98.7 us (99%)
  between operations  1.29 us (1%)
    pallas_call x1, Pallas kernels, on_device(): pl.pallas_call(kernel, out_shape=(jax.ShapeDtypeStruct((3, 4, 8, 8, 512),...  96.1 us
    pallas_call x1, Pallas kernels, on_device(): pl.pallas_call(spread, out_shape=(jax.ShapeDtypeStruct((RANK, D), F32), j...  2.58 us

profile of v4, /device:TPU:8, one launch (start us, length us, event | category | flops | bytes accessed | tf_op | source)
XLA Modules:
  0.0 99.9 jit_solution(5297920052509890465)
XLA Ops:
  1.3 96.1 %shard_map.95 = (bf16[3,4,8,8,512]{4,3,2,1,0:T(8,128)(2,1)}, bf16[4,8,8,384]{3,2,1,0:T(8,128)(2,1)}) custom-call(bf16[1,144,1536]{2,1,0:T(8,128)(2,1)} %frames.1, f32[1536]{0:T(1024)} %gain.1, bf16[48,384]{1,0:T(8,128)(2,1)} %w1.1, bf16[48,384]{1,0:T(8,128)(2,1)} %bitcast.9, bf16[64,1536]{1,0:T(8,128)(2,1)} %bitcast.8, bf16[1,64,6144]{2,1,0:T(8,128)(2,1)} %up_map.1, ...), custom_call_target="tpu_custom_call" | custom-call | tf_op jit(solution)/shard_map/pallas_call | solution.py:556
  97.4 2.6 %shard_map.96 = (f32[64,1536]{1,0:T(8,128)}, f32[64,6144]{1,0:T(8,128)}) custom-call(bf16[3,4,8,8,512]{4,3,2,1,0:T(8,128)(2,1)} %get-tuple-element.6.agu, bf16[4,8,8,384]{3,2,1,0:T(8,128)(2,1)} %get-tuple-element.7.agd), custom_call_target="tpu_custom_call" | custom-call | tf_op jit(solution)/shard_map/pallas_call | solution.py:589

commit v5 on v4

--- a/solution.py
+++ b/solution.py
@@ -21,12 +21,12 @@
 
 
 def kernel(
-    frames, gain, w1, w2t, down_map, up_map, lengths, cot,
-    agu, agd,
-    ws_a, ws_b, wa, wb, tok, ub, bks, bkr, bka, rss, rsr, dns, dnr,
+    frames_, gain, w1, w2t, down_map_, up_map, lengths, cot_,
+    ou, od,
+    agu, agd, ws_a, ws_b, wa, wb, tok, ub, bks, bkr, bka, rss, rsr, dns, dnr,
     ta_s, ta_r, tb_s, tb_r, tk_s, tk_r, td_s, td_r, u_s, u_r,
     az_s, az_r, bz_s, bz_r, by_s, by_r, bo_s, bo_r,
-    bk_s, bk_r, ba_s, ba_r, rs_s, rs_r, dn_s, dn_r, gz_s, gz_r, gx_s, gx_r,
+    bk_s, bk_r, ba_s, ba_r, rs_s, rs_r, dn_s, dn_r, gz_s, gz_r, gx_s, gx_r, o_s, frames, cot, down_map, i_s,
 ):
     fi = lax.axis_index("fsdp")
     mi = lax.axis_index("member")
@@ -58,6 +58,14 @@
 
     def got(ref, sem):
         rcopy(ref, ref, sem, sem, right).wait_recv()
+
+    fetch = [
+        pltpu.make_async_copy(frames_.at[:, 0:ROWS], frames, i_s.at[0]),
+        pltpu.make_async_copy(cot_.at[:, 0:ROWS], cot, i_s.at[1]),
+        pltpu.make_async_copy(down_map_, down_map, i_s.at[2]),
+    ]
+    for cp in fetch:
+        cp.start()
 
     barrier = pltpu.get_barrier_semaphore()
     peers = [up, dn, dev(x, yo, z, c), fore, aft, twin]
@@ -70,13 +78,8 @@
     for peer in peers:
         pl.semaphore_signal(barrier, inc=1, device_id=peer, device_id_type=MESH)
 
-    for e in range(1, 4):
-        peer = dev((x + e) % 4, x, z, c)
-        pl.semaphore_signal(barrier, inc=1, device_id=peer, device_id_type=MESH)
-
     @pl.when(x != y)
     def _():
-        pl.semaphore_signal(barrier, inc=1, device_id=dev(x, x, z, c), device_id_type=MESH)
         pl.semaphore_signal(barrier, inc=1, device_id=flip, device_id_type=MESH)
 
     ws_a[0] = w1[:, 0:128]
@@ -84,18 +87,22 @@
     ws_a[1] = w2t[:, 0:128]
     ws_b[1] = w2t[:, 128:384]
 
-    pl.semaphore_wait(barrier, len(peers) + jnp.where(x != y, 5, 3))
+    pl.semaphore_wait(barrier, len(peers) + jnp.where(x != y, 1, 0))
 
     def lanes(zh_):
         return pl.ds(pl.multiple_of(zh_ * 128, 128), 128)
 
-    def ta_copy(e):
-        to = dev(y, (y + e) % 4, z, c)
-        return rcopy(ws_a, wa.at[:, x, zl, :, lanes(zh)], ta_s.at[e], ta_r.at[x], to)
-
-    def ta_wait(a):
-        slot = wa.at[:, a, zl, :, lanes(zh)]
-        rcopy(slot, slot, ta_s.at[0], ta_r.at[a], flip).wait_recv()
+    def ta_slot(y_):
+        return wa.at[:, y_, zl, :, lanes(zh)]
+
+    def ta_copy():
+        return rcopy(ws_a, ta_slot(x), ta_s.at[0], ta_r.at[0], flip)
+
+    def ta_pass(e):
+        return rcopy(ta_slot(y), ta_slot(y), ta_s.at[1], ta_r.at[e], dev(x, (y + e) % 4, z, c))
+
+    def ta_wait(e):
+        got(ta_slot((y + 4 - e) % 4), ta_r.at[e])
 
     def tb_copy():
         return rcopy(ws_b, wb.at[zh, :, x, zl], tb_s.at[0], tb_r.at[0], flip)
@@ -103,7 +110,7 @@
     @pl.when(x != y)
     def _():
         tb_copy().start()
-        ta_copy(0).start()
+        ta_copy().start()
 
     @pl.when(x == y)
     def _():
@@ -111,9 +118,8 @@
             wa[w, y, zl, :, lanes(zh)] = ws_a[w]
             wb[zh, w, y, zl] = ws_b[w]
 
-    for e in range(1, 4):
-        ta_copy(e).start()
-
+    for cp in fetch:
+        cp.wait()
     v = frames[0, 0:ROWS, :].astype(F32)
     mean = jnp.mean(v, axis=1, keepdims=True)
     var = jnp.mean((v - mean) ** 2, axis=1, keepdims=True)
@@ -148,9 +154,9 @@
     for i in (0, 2, 1, 3):
         t_copy(i).start()
 
-    def a_str(s, w):
+    def a_str(s, e):
         z_ = (z + s + 16) % 16
-        return wa.at[w, :, z_ % 8, :, lanes(z_ // 8)]
+        return wa.at[:, (y + 4 - e) % 4, z_ % 8, :, lanes(z_ // 8)]
 
     def b_str(s, w):
         return b_half(s, y, w)
@@ -204,18 +210,19 @@
     for w in range(2):
         for route in range(2):
             z_copy(0, w, route, 1).start()
+    @pl.when(x != y)
+    def _():
+        ta_wait(0)
+
+    for e_ in range(1, 4):
+        ta_pass(e_).start()
     for way in range(2):
         by_copy(0, 0, way).start()
-    for e in range(1, 4):
-        ta_wait((x + e) % 4)
-
-    @pl.when(x != y)
-    def _():
-        ta_wait(x)
-
-    for w in range(2):
+    for e in range(4):
+        if e > 0:
+            ta_wait(e)
         for route in range(2):
-            z_copy(1, w, route, 1).start()
+            z_copy(1, e, route, 1).start()
 
     for h in range(2):
         d_copy(0, h).start()
@@ -246,10 +253,10 @@
         for route in range(2):
             for way in range(2):
                 by_copy(-k if route == 0 else k, 2 * k - 1 + route, way).start()
-        for w in range(2):
+        for e in range(4):
             for route in range(2):
-                z_wait(1, w, route, k)
-                z_copy(1, w, route, k + 1).start()
+                z_wait(1, e, route, k)
+                z_copy(1, e, route, k + 1).start()
         for route in range(2):
             s = -(k - 1) if route == 0 else (k - 1)
 
@@ -278,11 +285,11 @@
     for route in range(2):
         for way in range(2):
             by_copy(-7 if route == 0 else 7, 13 + route, way).start()
-    for w in range(2):
+    for e in range(4):
         for route in range(2):
-            z_wait(1, w, route, 7)
-            if route == w:
-                z_copy(1, w, route, 8).start()
+            z_wait(1, e, route, 7)
+            if route == e // 2:
+                z_copy(1, e, route, 8).start()
     y_stage(-6, 11)
     y_stage(6, 12)
     for w in range(2):
@@ -294,13 +301,9 @@
     for i in (4, 5):
         t_wait(i)
         d_copy(3, i - 4).start()
-    for w in range(2):
-        z_wait(1, w, w, 8)
-    for way in range(3):
-        by_last_wait(way)
-
-    for way in range(2):
-        got(wb.at[0, 0, 0:3, 0:5], bo_r.at[way])
+    for e in range(4):
+        z_wait(1, e, e // 2, 8)
+
     got(tok.at[:, 0], td_r.at[0])
     for zh_ in range(2):
         u_local(zh_).wait()
@@ -324,7 +327,7 @@
                 rss[g, m, r] = part[8 * r : 8 * r + 8].astype(BF16)
             for x_ in range(4):
                 bp = dot(u, dpre[ROWS * x_ : ROWS * (x_ + 1)], ((1,), (1,)))
-                if g == 0:
+                if g == 2:
                     bks[x_, m] = bp
                 else:
                     bks[x_, m] += bp
@@ -436,16 +439,20 @@
         gx_wait(g, 2)
         gx_copy(g, 5).start()
 
+    third(2)
+    rs_start(2)
+    for way in range(3):
+        by_last_wait(way)
+    for way in range(2):
+        got(wb.at[0, 0, 0:3, 0:5], bo_r.at[way])
     third(0)
     rs_start(0)
     third(1)
-    rs_start(1)
-    third(2)
     for d in range(1, 4):
         for c_ in range(2):
             bk_copy(d, c_).start()
     bk_other().start()
-    rs_start(2)
+    rs_start(1)
     bkr[x, c] = bks[x, c]
 
     got(bkr.at[x, 1 - c], bk_r.at[2])
@@ -458,10 +465,10 @@
     for d in range(1, 4):
         ba_copy(d).start()
 
+    rs_sum(2)
+    gz_own(2)
     rs_sum(0)
     gz_own(0)
-    rs_sum(1)
-    gz_own(1)
 
     got(bka.at[0:3], ba_r.at[0])
     quarter = pl.ds(pl.multiple_of(x * 384, 128), 384)
@@ -474,41 +481,44 @@
         dn_copy(d).start()
     dnr[zl] = dns[zl]
 
-    rs_sum(2)
-    gz_all(2)
+    rs_sum(1)
+    gz_own(1)
+    gz_pass(2)
+    gx_first(2)
     gz_pass(0)
     gx_first(0)
-    gz_pass(1)
-    gx_first(1)
-    gx_second(0)
+    gx_second(2)
     got(dnr.at[0:7], dn_r.at[0])
     total = dnr[0].astype(F32)
     for i in range(1, 8):
         total = total + dnr[i].astype(F32)
     agd[x, zl] = total.astype(BF16)
     gz_all(3)
+    gz_pass(1)
+    gx_second(0)
+    gx_pass(2)
+    gx_first(1)
     gx_second(1)
     gx_pass(0)
-    gz_all_wait(2)
-    for i in (0, 2, 3, 1):
-        gx_copy(2, i).start()
-    gx_pass(1)
     gz_all_wait(3)
     for d in range(1, 4):
         gd_copy(d).start()
-    gx_pass(2)
-    for g in range(3):
+    gx_pass(1)
+    outs = [pltpu.make_async_copy(agu.at[g], ou.at[g], o_s.at[g]) for g in range(3)]
+    outs.append(pltpu.make_async_copy(agd, od, o_s.at[3]))
+    for g in (2, 0, 1):
         for i in (1, 3, 4, 5):
             gx_wait(g, i)
+        outs[g].start()
     got(agd.at[0:3], gx_r.at[3, 0])
+    outs[3].start()
 
     @pl.when(x != y)
     def _():
         tb_copy().wait_send()
-        ta_copy(0).wait_send()
-
-    for e in range(1, 4):
-        ta_copy(e).wait_send()
+        ta_copy().wait_send()
+
+    sent(wa.at[:, 0:3, 0, :, 0:128], ta_s.at[1])
     sent(tok.at[0:3, 0], tk_s.at[0])
     sent(tok.at[:, 0], td_s.at[0])
     for zh_ in range(2):
@@ -532,6 +542,8 @@
         sent(agu.at[g, 0:3], gx_s.at[g])
     sent(agd.at[0, 0:7], gz_s.at[3])
     sent(agd.at[0:3], gx_s.at[3])
+    for out in outs:
+        out.wait()
 
 
 def spread(agu, agd, dn_out, up_out):
@@ -552,6 +564,7 @@
 
 def on_device(frames, gain, w1, w2, down_map, up_map, lengths, cot):
     vmem = pl.BlockSpec(memory_space=pltpu.VMEM)
+    hbm = pl.BlockSpec(memory_space=pl.ANY)
     dma = pltpu.SemaphoreType.DMA
     pieces = pl.pallas_call(
         kernel,
@@ -559,10 +572,11 @@
             jax.ShapeDtypeStruct((3, 4, 8, 8, 512), BF16),
             jax.ShapeDtypeStruct((4, 8, 8, 384), BF16),
         ),
-        in_specs=[vmem, vmem, vmem, vmem, vmem, pl.BlockSpec(memory_space=pl.ANY),
-                  pl.BlockSpec(memory_space=pltpu.SMEM), vmem],
-        out_specs=(vmem, vmem),
+        in_specs=[hbm, vmem, vmem, vmem, hbm, hbm, pl.BlockSpec(memory_space=pltpu.SMEM), hbm],
+        out_specs=(pl.BlockSpec(memory_space=pl.ANY), pl.BlockSpec(memory_space=pl.ANY)),
         scratch_shapes=[
+            pltpu.VMEM((3, 4, 8, 8, 512), BF16),
+            pltpu.VMEM((4, 8, 8, 384), BF16),
             pltpu.VMEM((2, 48, 128), BF16),
             pltpu.VMEM((2, 48, 256), BF16),
             pltpu.VMEM((2, 4, 8, 48, 256), BF16),
@@ -577,10 +591,14 @@
             pltpu.VMEM((8, 8, 384), BF16),
             pltpu.VMEM((8, 8, 384), BF16),
             dma((4,)), dma((4,)), dma((1,)), dma((1,)), dma((1,)), dma((6,)), dma((1,)), dma((1,)), dma((4,)), dma((2,)),
-            dma((2,)), dma((2, 2, 8)), dma((2,)), dma((2, 2, 8)),
+            dma((2,)), dma((2, 4, 8)), dma((2,)), dma((2, 2, 8)),
             dma((3,)), dma((3, 16)), dma((2,)), dma((2,)),
             dma((3,)), dma((3,)), dma((1,)), dma((1,)), dma((3, 3)), dma((3, 3)),
-            dma((1,)), dma((1,)), dma((4,)), dma((4, 3)), dma((4,)), dma((4, 6)),
+            dma((1,)), dma((1,)), dma((4,)), dma((4, 3)), dma((4,)), dma((4, 6)), dma((4,)),
+            pltpu.VMEM((1, ROWS, D), BF16),
+            pltpu.VMEM((1, ROWS, D), BF16),
+            pltpu.VMEM((RANK, D), BF16),
+            dma((3,)),
         ],
         compiler_params=pltpu.CompilerParams(
             collective_id=0, has_side_effects=True, vmem_limit_bytes=56 * 1024 * 1024

time: 100 us -> 96.1 us (0.961)
  the two profiles are of different devices: /device:TPU:8 before, /device:TPU:2 now
where the time goes in v5:
time: 96.1 us; the launch traced here: 95.9 us
  Pallas kernels  94.6 us (98%)
  between operations  1.29 us (1%)
    pallas_call x1, Pallas kernels, on_device(): pl.pallas_call(kernel, out_shape=(jax.ShapeDtypeStruct((3, 4, 8, 8, 512),...  92.1 us
    pallas_call x1, Pallas kernels, on_device(): pl.pallas_call(spread, out_shape=(jax.ShapeDtypeStruct((RANK, D), F32), j...  2.58 us

profile of v5, /device:TPU:2, one launch (start us, length us, event | category | flops | bytes accessed | tf_op | source)
XLA Modules:
  0.0 95.9 jit_solution(18064578046271279194)
XLA Ops:
  1.3 92.1 %shard_map.95 = (bf16[3,4,8,8,512]{4,3,2,1,0:T(8,128)(2,1)}, bf16[4,8,8,384]{3,2,1,0:T(8,128)(2,1)}) custom-call(bf16[1,144,1536]{2,1,0:T(8,128)(2,1)} %frames_.1, f32[1536]{0:T(1024)} %gain.1, bf16[48,384]{1,0:T(8,128)(2,1)} %w1.1, bf16[48,384]{1,0:T(8,128)(2,1)} %bitcast.9, bf16[64,1536]{1,0:T(8,128)(2,1)} %bitcast.8, bf16[1,64,6144]{2,1,0:T(8,128)(2,1)} %up_map.1, ...), custom_call_target="tpu_custom_call" | custom-call | tf_op jit(solution)/shard_map/pallas_call | solution.py:569
  93.3 2.6 %shard_map.96 = (f32[64,1536]{1,0:T(8,128)}, f32[64,6144]{1,0:T(8,128)}) custom-call(bf16[3,4,8,8,512]{4,3,2,1,0:T(8,128)(2,1)} %get-tuple-element.6.agu, bf16[4,8,8,384]{3,2,1,0:T(8,128)(2,1)} %get-tuple-element.7.agd), custom_call_target="tpu_custom_call" | custom-call | tf_op jit(solution)/shard_map/pallas_call | solution.py:607

commit v6 on v5

--- a/solution.py
+++ b/solution.py
@@ -485,15 +485,15 @@
     gz_own(1)
     gz_pass(2)
     gx_first(2)
-    gz_pass(0)
-    gx_first(0)
-    gx_second(2)
     got(dnr.at[0:7], dn_r.at[0])
     total = dnr[0].astype(F32)
     for i in range(1, 8):
         total = total + dnr[i].astype(F32)
     agd[x, zl] = total.astype(BF16)
     gz_all(3)
+    gz_pass(0)
+    gx_first(0)
+    gx_second(2)
     gz_pass(1)
     gx_second(0)
     gx_pass(2)

time: 96.1 us -> 95.9 us (level)
  no operation moved by 1% of the time
where the time goes in v6:
time: 95.9 us; the launch traced here: 95.7 us
  Pallas kernels  94.4 us (98%)
  between operations  1.29 us (1%)
    pallas_call x1, Pallas kernels, on_device(): pl.pallas_call(kernel, out_shape=(jax.ShapeDtypeStruct((3, 4, 8, 8, 512),...  91.8 us
    pallas_call x1, Pallas kernels, on_device(): pl.pallas_call(spread, out_shape=(jax.ShapeDtypeStruct((RANK, D), F32), j...  2.58 us

profile of v6, /device:TPU:2, one launch (start us, length us, event | category | flops | bytes accessed | tf_op | source)
XLA Modules:
  0.0 95.7 jit_solution(680253115264192352)
XLA Ops:
  1.3 91.8 %shard_map.95 = (bf16[3,4,8,8,512]{4,3,2,1,0:T(8,128)(2,1)}, bf16[4,8,8,384]{3,2,1,0:T(8,128)(2,1)}) custom-call(bf16[1,144,1536]{2,1,0:T(8,128)(2,1)} %frames_.1, f32[1536]{0:T(1024)} %gain.1, bf16[48,384]{1,0:T(8,128)(2,1)} %w1.1, bf16[48,384]{1,0:T(8,128)(2,1)} %bitcast.9, bf16[64,1536]{1,0:T(8,128)(2,1)} %bitcast.8, bf16[1,64,6144]{2,1,0:T(8,128)(2,1)} %up_map.1, ...), custom_call_target="tpu_custom_call" | custom-call | tf_op jit(solution)/shard_map/pallas_call | solution.py:569
  93.1 2.6 %shard_map.96 = (f32[64,1536]{1,0:T(8,128)}, f32[64,6144]{1,0:T(8,128)}) custom-call(bf16[3,4,8,8,512]{4,3,2,1,0:T(8,128)(2,1)} %get-tuple-element.6.agu, bf16[4,8,8,384]{3,2,1,0:T(8,128)(2,1)} %get-tuple-element.7.agd), custom_call_target="tpu_custom_call" | custom-call | tf_op jit(solution)/shard_map/pallas_call | solution.py:607
